TPU v7x, 32 devices: a whole 2x2x4 slice. The times are simulated.
32 devices in a mesh: dp: 8 (over y, x, core), tensor: 4 (over z).
Axes of the slice: x: 2, y: 2, z: 4, core: 2. Of those that a mesh axis runs over, the one named last changes fastest.
Arguments:
- x_in: float32 [4096, 1024], P(('dp', 'tensor')), may hold values from -6 to 6
- d_out: float32 [4096, 1024], P(('dp', 'tensor')), may hold values from -6 to 6
- seq_lengths: int32 [8, 2], P('dp'), may hold values from 128 to 384, as said below
- w_qkv: bfloat16 [2, 1024, 3, 1024], P(None, 'dp', None, 'tensor'), may hold values from -0.1875 to 0.1875
- b_qv: bfloat16 [2, 2, 1024], P(None, None, ('tensor', 'dp')), may hold values from -3 to 3
- w_o: bfloat16 [2, 1024, 1024], P(None, 'tensor', 'dp'), may hold values from -0.5 to 0.5
- w_1: bfloat16 [2, 1024, 4096], P(None, 'dp', 'tensor'), may hold values from -0.1875 to 0.1875
- b_ffn: bfloat16 [2, 4096], P(None, ('tensor', 'dp')), may hold values from -3 to 3
- w_2: bfloat16 [2, 4096, 1024], P(None, 'tensor', 'dp'), may hold values from -0.09375 to 0.09375
- norm_gains: bfloat16 [2, 2, 1024], P(None, None, 'dp'), may hold values from 0.5 to 1.5
- vec_biases: bfloat16 [2, 4, 1024], P(None, None, 'dp'), may hold values from -3 to 3
Outputs:
- output: float32 [4096, 1024], P(('dp', 'tensor'))
- grad_x: float32 [4096, 1024], P(('dp', 'tensor'))
- grad_w_qkv: float32 [2, 1024, 3, 1024], P(None, 'dp', None, 'tensor')
- grad_b_qv: float32 [2, 2, 1024], P(None, None, ('tensor', 'dp'))
- grad_w_o: float32 [2, 1024, 1024], P(None, 'tensor', 'dp')
- grad_w_1: float32 [2, 1024, 4096], P(None, 'dp', 'tensor')
- grad_b_ffn: float32 [2, 4096], P(None, ('tensor', 'dp'))
- grad_w_2: float32 [2, 4096, 1024], P(None, 'tensor', 'dp')
- grad_norm_gains: float32 [2, 2, 1024], P(None, None, 'dp')
- grad_vec_biases: float32 [2, 4, 1024], P(None, None, 'dp')
Inputs may be any that keep to these rules, and one draw needn't show every extreme that they name: `seq_lengths`: each row lists the lengths of the 2 sequences of one group in packing order; they sum to 512. Some group holds a sequence of length exactly 384.
All inputs are finite; a program needn't handle non-finite values.
Results may differ from a plain program's by a relative error of at most 0.02.
Values may be sent and summed in bfloat16 or wider, within the bound.
A program may use at most 128 MiB of HBM per device.

v0:
```python
import math

import jax
import jax.numpy as jnp
from jax import lax
from jax.sharding import PartitionSpec as P

HEAD_DIM = 64


NORM_EPS = 1e-05
GELU_COEFF = 0.7978845608028654
GELU_CUBIC = 0.044715


def layer_norm(inputs, gain_row, bias_row):
    row_mean = jnp.mean(inputs, axis=-1, keepdims=True)
    centered = inputs - row_mean
    inv_std = lax.rsqrt(jnp.mean(centered * centered, axis=-1, keepdims=True) + NORM_EPS)
    normed = centered * inv_std
    return (normed * gain_row + bias_row, normed, inv_std)


def norm_back(grad_in, normed, inv_std, gain_row):
    scaled = grad_in * gain_row
    return inv_std * (
        scaled
        - jnp.mean(scaled, axis=-1, keepdims=True)
        - normed * jnp.mean(scaled * normed, axis=-1, keepdims=True)
    )


def gelu_pair(pre_act):
    squared = pre_act * pre_act
    tangent = jnp.tanh(GELU_COEFF * (pre_act + GELU_CUBIC * squared * pre_act))
    gelu_value = 0.5 * pre_act * (1.0 + tangent)
    gelu_slope = 0.5 * (1.0 + tangent) + 0.5 * pre_act * (1.0 - tangent * tangent) * GELU_COEFF * (
        1.0 + 3.0 * GELU_CUBIC * squared
    )
    return (gelu_value, gelu_slope)


def segment_ids(lengths, total_rows):
    sequence_ends = jnp.cumsum(lengths)
    positions = jnp.arange(total_rows, dtype=jnp.int32)
    return jnp.sum(
        (positions[:, None] >= sequence_ends[None, :]).astype(jnp.int32), axis=1, dtype=jnp.int32
    )


def contract_first(left, right):
    return lax.dot_general(
        left, right, (((0,), (0,)), ((), ())), preferred_element_type=jnp.float32
    )


def contract_last(left, right):
    return lax.dot_general(
        left, right, (((1,), (1,)), ((), ())), preferred_element_type=jnp.float32
    )


def block_scores(query_block, key_vecs, segments, row_start, block_rows, score_scale):
    positions = jnp.arange(key_vecs.shape[0], dtype=jnp.int32)
    query_pos = row_start + jnp.arange(block_rows, dtype=jnp.int32)
    allowed = (segments[:, None] == segments[None, :]) & (positions[None, :] <= query_pos[:, None])
    scores = (
        jnp.einsum("qhd,khd->hqk", query_block, key_vecs, preferred_element_type=jnp.float32)
        * score_scale
    )
    return jnp.where(allowed[None], scores, -jnp.inf)


def attend(queries, key_vecs, val_vecs, segments, score_scale):
    group_rows = queries.shape[0]
    block_rows = min(group_rows, 512)

    def one_block(block_index):
        row_start = block_index * block_rows
        scores = block_scores(queries, key_vecs, segments, row_start, block_rows, score_scale)
        row_max = jnp.max(scores, axis=-1, keepdims=True)
        log_total = row_max + jnp.log(jnp.sum(jnp.exp(scores - row_max), axis=-1, keepdims=True))
        probs_half = jnp.exp(scores - log_total).astype(jnp.bfloat16)
        attended = jnp.einsum(
            "hqk,khd->qhd", probs_half, val_vecs, preferred_element_type=jnp.float32
        )
        return (attended.astype(jnp.bfloat16), log_total[..., 0])

    attended, log_total = lax.map(one_block, jnp.arange(group_rows // block_rows, dtype=jnp.int32))
    return (attended.reshape(group_rows, -1), log_total)


def attend_back(queries, key_vecs, val_vecs, grad_attended, log_total, segments, score_scale):
    group_rows = queries.shape[0]
    block_rows = min(group_rows, 512)

    def one_block(totals, block_index):
        key_grad, val_grad = totals
        row_start = block_index * block_rows
        scores = block_scores(queries, key_vecs, segments, row_start, block_rows, score_scale)
        soft_probs = jnp.exp(scores - log_total[block_index][..., None])
        probs_half = soft_probs.astype(jnp.bfloat16)
        grad_probs = jnp.einsum(
            "qhd,khd->hqk", grad_attended, val_vecs, preferred_element_type=jnp.float32
        )
        val_grad = val_grad + jnp.einsum(
            "hqk,qhd->khd", probs_half, grad_attended, preferred_element_type=jnp.float32
        )
        row_dot = jnp.sum(grad_probs * soft_probs, axis=-1, keepdims=True)
        score_grad = (soft_probs * (grad_probs - row_dot) * score_scale).astype(jnp.bfloat16)
        query_grad = jnp.einsum(
            "hqk,khd->qhd", score_grad, key_vecs, preferred_element_type=jnp.float32
        )
        key_grad = key_grad + jnp.einsum(
            "hqk,qhd->khd", score_grad, queries, preferred_element_type=jnp.float32
        )
        return ((key_grad, val_grad), query_grad)

    empty = jnp.zeros(queries.shape, jnp.float32)
    (key_grad, val_grad), query_grads = lax.scan(
        one_block, (empty, empty), jnp.arange(group_rows // block_rows, dtype=jnp.int32)
    )
    return (query_grads.reshape(queries.shape), key_grad, val_grad)


def shards(x_in, d_out, seq_lengths, w_qkv, b_qv, w_o, w_1, b_ffn, w_2, norm_gains, vec_biases):
    own_rows = x_in.shape[0]
    group_rows = own_rows * lax.axis_size("tensor")
    layer_count = w_qkv.shape[0]
    score_scale = 1.0 / math.sqrt(HEAD_DIM)
    segments = segment_ids(seq_lengths[0], group_rows)

    def fetch(layer_index):
        return (
            lax.all_gather(w_qkv[layer_index], "dp", axis=0, tiled=True),
            lax.all_gather(w_o[layer_index], "dp", axis=1, tiled=True),
            lax.all_gather(w_1[layer_index], "dp", axis=0, tiled=True),
            lax.all_gather(w_2[layer_index], "dp", axis=1, tiled=True),
            lax.all_gather(b_qv[layer_index], "dp", axis=1, tiled=True),
            lax.all_gather(b_ffn[layer_index], "dp", axis=0, tiled=True),
            lax.all_gather(norm_gains[layer_index], "dp", axis=1, tiled=True),
            lax.all_gather(vec_biases[layer_index], "dp", axis=1, tiled=True),
        )

    def collect(own_part):
        return lax.all_gather(own_part, "tensor", axis=0, tiled=True)

    def collect_grad(own_part):
        return lax.all_gather(own_part, "tensor", axis=0, tiled=True)

    def reduce_rows(left, right):

        def term(row_start, row_count):
            return jnp.dot(left, right, preferred_element_type=jnp.float32)

        return lax.psum_scatter(
            term(jnp.int32(0), own_rows * lax.axis_size("tensor")).astype(jnp.bfloat16),
            "tensor",
            scatter_dimension=0,
            tiled=True,
        ).astype(jnp.float32)

    def reduce_back(left, right):

        def term(row_start, row_count):
            return contract_last(left, right)

        return lax.psum_scatter(
            term(jnp.int32(0), own_rows * lax.axis_size("tensor")).astype(jnp.bfloat16),
            "tensor",
            scatter_dimension=0,
            tiled=True,
        ).astype(jnp.float32)

    kept = []
    caches = []
    hidden_in = x_in
    for layer_index in range(layer_count):
        fetched = fetch(layer_index)
        kept.append(fetched)
        qkv_weight, out_weight, up_weight, down_weight, qv_bias, up_bias, gain_rows, bias_rows = (
            fetched
        )
        gain_rows = gain_rows.astype(jnp.float32)
        bias_rows = bias_rows.astype(jnp.float32)
        width = qkv_weight.shape[0]
        local_width = qkv_weight.shape[2]
        local_heads = local_width // HEAD_DIM
        normed_own, unit_one, inv_one = layer_norm(hidden_in, gain_rows[0], bias_rows[0])
        normed_one = collect(normed_own.astype(jnp.bfloat16))
        projected = jnp.dot(
            normed_one,
            qkv_weight.reshape(width, 3 * local_width),
            preferred_element_type=jnp.float32,
        ).reshape(group_rows, 3, local_width)
        bias_float = qv_bias.astype(jnp.float32)
        queries = (
            (projected[:, 0] + bias_float[0])
            .astype(jnp.bfloat16)
            .reshape(group_rows, local_heads, HEAD_DIM)
        )
        key_vecs = projected[:, 1].astype(jnp.bfloat16).reshape(group_rows, local_heads, HEAD_DIM)
        val_vecs = (
            (projected[:, 2] + bias_float[1])
            .astype(jnp.bfloat16)
            .reshape(group_rows, local_heads, HEAD_DIM)
        )
        attended, log_total = attend(queries, key_vecs, val_vecs, segments, score_scale)
        residual_mid = hidden_in + reduce_rows(attended, out_weight) + bias_rows[2]
        normed_own_two, unit_two, inv_two = layer_norm(residual_mid, gain_rows[1], bias_rows[1])
        normed_two = collect(normed_own_two.astype(jnp.bfloat16))
        pre_act = jnp.dot(
            normed_two, up_weight, preferred_element_type=jnp.float32
        ) + up_bias.astype(jnp.float32)
        gelu_value, gelu_slope = gelu_pair(pre_act)
        activated = gelu_value.astype(jnp.bfloat16)
        hidden_out = residual_mid + reduce_rows(activated, down_weight) + bias_rows[3]
        caches.append(
            (
                unit_one,
                inv_one,
                normed_one,
                queries,
                key_vecs,
                val_vecs,
                attended,
                log_total,
                unit_two,
                inv_two,
                normed_two,
                activated,
                gelu_slope,
            )
        )
        hidden_in = hidden_out
    back = d_out
    owned_grads = [None] * layer_count
    for layer_index in reversed(range(layer_count)):
        fetched = fetch(layer_index)
        qkv_weight, out_weight, up_weight, down_weight, qv_bias, up_bias, gain_rows, bias_rows = (
            fetched
        )
        gain_rows = gain_rows.astype(jnp.float32)
        width = qkv_weight.shape[0]
        local_width = qkv_weight.shape[2]
        local_heads = local_width // HEAD_DIM
        (
            unit_one,
            inv_one,
            normed_one,
            queries,
            key_vecs,
            val_vecs,
            attended,
            log_total,
            unit_two,
            inv_two,
            normed_two,
            activated,
            gelu_slope,
        ) = caches[layer_index]
        grad_half = collect_grad(back.astype(jnp.bfloat16))
        grad_down = contract_first(activated, grad_half)
        grad_pre = contract_last(grad_half, down_weight) * gelu_slope
        grad_pre_half = grad_pre.astype(jnp.bfloat16)
        grad_up = contract_first(normed_two, grad_pre_half)
        grad_normed_two = reduce_back(grad_pre_half, up_weight)
        grad_mid = back + norm_back(grad_normed_two, unit_two, inv_two, gain_rows[1])
        grad_mid_half = collect_grad(grad_mid.astype(jnp.bfloat16))
        grad_out_proj = contract_first(attended, grad_mid_half)
        grad_attended = contract_last(grad_mid_half, out_weight).astype(jnp.bfloat16)
        grad_attended = grad_attended.reshape(group_rows, local_heads, HEAD_DIM)
        query_grad, key_grad, val_grad = attend_back(
            queries, key_vecs, val_vecs, grad_attended, log_total, segments, score_scale
        )
        grad_qkv = jnp.stack([query_grad, key_grad, val_grad], axis=1).astype(jnp.bfloat16)
        grad_qkv = grad_qkv.reshape(group_rows, 3 * local_width)
        grad_qv_bias = jnp.stack(
            [
                jnp.sum(query_grad, axis=0).reshape(local_width),
                jnp.sum(val_grad, axis=0).reshape(local_width),
            ]
        )
        grad_qkv_weight = contract_first(normed_one, grad_qkv).reshape(width, 3, local_width)
        grad_normed_one = reduce_back(grad_qkv, qkv_weight.reshape(width, 3 * local_width))
        next_back = grad_mid + norm_back(grad_normed_one, unit_one, inv_one, gain_rows[0])
        grad_gains = jnp.stack(
            [
                jnp.sum(grad_normed_one * unit_one, axis=0),
                jnp.sum(grad_normed_two * unit_two, axis=0),
            ]
        )
        grad_vbias = jnp.stack(
            [
                jnp.sum(grad_normed_one, axis=0),
                jnp.sum(grad_normed_two, axis=0),
                jnp.sum(grad_mid, axis=0),
                jnp.sum(back, axis=0),
            ]
        )
        layer_terms = (
            grad_qkv_weight,
            grad_out_proj,
            grad_up,
            grad_down,
            grad_qv_bias,
            jnp.sum(grad_pre, axis=0),
            grad_gains,
            grad_vbias,
        )
        owned_grads[layer_index] = (
            lax.psum_scatter(
                layer_terms[0].astype(jnp.bfloat16), "dp", scatter_dimension=0, tiled=True
            ).astype(jnp.float32),
            lax.psum_scatter(
                layer_terms[1].astype(jnp.bfloat16), "dp", scatter_dimension=1, tiled=True
            ).astype(jnp.float32),
            lax.psum_scatter(
                layer_terms[2].astype(jnp.bfloat16), "dp", scatter_dimension=0, tiled=True
            ).astype(jnp.float32),
            lax.psum_scatter(
                layer_terms[3].astype(jnp.bfloat16), "dp", scatter_dimension=1, tiled=True
            ).astype(jnp.float32),
            lax.psum_scatter(
                layer_terms[4].astype(jnp.bfloat16), "dp", scatter_dimension=1, tiled=True
            ).astype(jnp.float32),
            lax.psum_scatter(
                layer_terms[5].astype(jnp.bfloat16), "dp", scatter_dimension=0, tiled=True
            ).astype(jnp.float32),
            lax.psum_scatter(
                layer_terms[6].astype(jnp.bfloat16), "dp", scatter_dimension=1, tiled=True
            ).astype(jnp.float32),
            lax.psum_scatter(
                layer_terms[7].astype(jnp.bfloat16), "dp", scatter_dimension=1, tiled=True
            ).astype(jnp.float32),
        )
        back = next_back
    stacked = tuple(
        (
            jnp.stack([owned_grads[index][member] for index in range(layer_count)])
            for member in range(8)
        )
    )
    gain_total, bias_total = lax.psum((stacked[6], stacked[7]), "tensor")
    return (
        hidden_in,
        back,
        stacked[0],
        stacked[4],
        stacked[1],
        stacked[2],
        stacked[5],
        stacked[3],
        gain_total,
        bias_total,
    )


def solution(mesh):
    in_specs = (
        P(("dp", "tensor"), None),
        P(("dp", "tensor"), None),
        P("dp", None),
        P(None, "dp", None, "tensor"),
        P(None, None, ("tensor", "dp")),
        P(None, "tensor", "dp"),
        P(None, "dp", "tensor"),
        P(None, ("tensor", "dp")),
        P(None, "tensor", "dp"),
        P(None, None, "dp"),
        P(None, None, "dp"),
    )
    out_specs = (
        P(("dp", "tensor"), None),
        P(("dp", "tensor"), None),
        P(None, "dp", None, "tensor"),
        P(None, None, ("tensor", "dp")),
        P(None, "tensor", "dp"),
        P(None, "dp", "tensor"),
        P(None, ("tensor", "dp")),
        P(None, "tensor", "dp"),
        P(None, None, "dp"),
        P(None, None, "dp"),
    )
    return jax.shard_map(shards, mesh=mesh, in_specs=in_specs, out_specs=out_specs, check_vma=False)
```

profile of v0, /device:TPU:0, one launch (start us, length us, event | category | flops | bytes accessed | tf_op | source)
XLA Modules:
  0.0 1320.1 jit_solution(2534194683769511238)
XLA Ops:
  60.7 27.6 %all-gather.47.cloned.1.call-done = bf16[1,1024,3,256]{1,3,2,0:T(8,128)(2,1)} async-done(((bf16[1,128,3,256]{1,3,2,0:T(8,128)(2,1)}), bf16[1,1024,3,256]{1,3,2,0:T(8,128)(2,1)}) %all-gather.47.cloned.1.call-update) | async-done | bytes 1572880 | tf_op jit(solution)/shard_map/all_gather | solution.py:135
  98.5 26.5 %reduce-scatter.43.cloned.1.call-done = bf16[128,1024]{1,0:T(8,128)(2,1)} async-done(((bf16[512,1024]{1,0:T(8,128)(2,1)}), bf16[128,1024]{1,0:T(8,128)(2,1)}) %reduce-scatter.43.cloned.1.call-update) | async-done | bytes 262160 | tf_op jit(solution)/shard_map/reduce_scatter | solution.py:156
  137.0 16.6 %all-gather.49.cloned.1.call-done = bf16[1,1024,1024]{2,1,0:T(8,128)(2,1)} async-done(((bf16[1,128,1024]{2,1,0:T(8,128)(2,1)}), bf16[1,1024,1024]{2,1,0:T(8,128)(2,1)}) %all-gather.49.cloned.1.call-update) | async-done | bytes 2097168 | tf_op jit(solution)/shard_map/all_gather | solution.py:137
  153.6 30.0 %all-gather.33.cloned.1.call-done = bf16[512,1024]{1,0:T(8,128)(2,1)} async-done(((bf16[128,1024]{1,0:T(8,128)(2,1)}), bf16[512,1024]{1,0:T(8,128)(2,1)}) %all-gather.33.cloned.1.call-update) | async-done | bytes 1048592 | tf_op jit(solution)/shard_map/all_gather | solution.py:146
  188.1 25.3 %all-gather.51.cloned.1.call-done = bf16[1,1024,1024]{2,1,0:T(8,128)(2,1)} async-done(((bf16[1,1024,128]{2,1,0:T(8,128)(2,1)}), bf16[1,1024,1024]{2,1,0:T(8,128)(2,1)}) %all-gather.51.cloned.1.call-update) | async-done | bytes 2097168 | tf_op jit(solution)/shard_map/all_gather | solution.py:138
  273.7 29.5 %all-gather.35.cloned.1.call-done = bf16[512,1024]{1,0:T(8,128)(2,1)} async-done(((bf16[128,1024]{1,0:T(8,128)(2,1)}), bf16[512,1024]{1,0:T(8,128)(2,1)}) %all-gather.35.cloned.1.call-update) | async-done | bytes 1048592 | tf_op jit(solution)/shard_map/all_gather | solution.py:146
  313.2 26.0 %reduce-scatter.47.cloned.1.call-done = bf16[128,1024]{1,0:T(8,128)(2,1)} async-done(((bf16[512,1024]{1,0:T(8,128)(2,1)}), bf16[128,1024]{1,0:T(8,128)(2,1)}) %reduce-scatter.47.cloned.1.call-update) | async-done | bytes 262160 | tf_op jit(solution)/shard_map/reduce_scatter | solution.py:156
  351.7 16.3 %all-gather.55.cloned.1.call-done = bf16[1,1024,1024]{2,1,0:T(8,128)(2,1)} async-done(((bf16[1,128,1024]{2,1,0:T(8,128)(2,1)}), bf16[1,1024,1024]{2,1,0:T(8,128)(2,1)}) %all-gather.55.cloned.1.call-update) | async-done | bytes 2097168 | tf_op jit(solution)/shard_map/all_gather | solution.py:137
  368.1 30.0 %all-gather.37.cloned.1.call-done = bf16[512,1024]{1,0:T(8,128)(2,1)} async-done(((bf16[128,1024]{1,0:T(8,128)(2,1)}), bf16[512,1024]{1,0:T(8,128)(2,1)}) %all-gather.37.cloned.1.call-update) | async-done | bytes 1048592 | tf_op jit(solution)/shard_map/all_gather | solution.py:146
  402.5 25.1 %all-gather.39.cloned.1.call-done = bf16[512,1024]{1,0:T(8,128)(2,1)} async-done(((bf16[128,1024]{1,0:T(8,128)(2,1)}), bf16[512,1024]{1,0:T(8,128)(2,1)}) %all-gather.39.cloned.1.call-update) | async-done | bytes 1048592 | tf_op jit(solution)/shard_map/all_gather | solution.py:149
  427.6 29.8 %all-gather.57.cloned.1.call-done = bf16[1,1024,1024]{2,1,0:T(8,128)(2,1)} async-done(((bf16[1,1024,128]{2,1,0:T(8,128)(2,1)}), bf16[1,1024,1024]{2,1,0:T(8,128)(2,1)}) %all-gather.57.cloned.1.call-update) | async-done | bytes 2097168 | tf_op jit(solution)/shard_map/all_gather | solution.py:138
  470.5 22.6 %reduce-scatter.51.cloned.1.call-done = bf16[128,1024]{1,0:T(8,128)(2,1)} async-done(((bf16[512,1024]{1,0:T(8,128)(2,1)}), bf16[128,1024]{1,0:T(8,128)(2,1)}) %reduce-scatter.51.cloned.1.call-update) | async-done | bytes 262160 | tf_op jit(solution)/shard_map/reduce_scatter | solution.py:168
  494.4 27.3 %reduce-scatter.49.cloned.1.call-done = bf16[128,1024]{1,0:T(8,128)(2,1)} async-done(((bf16[512,1024]{1,0:T(8,128)(2,1)}), bf16[128,1024]{1,0:T(8,128)(2,1)}) %reduce-scatter.49.cloned.1.call-update) | async-done | bytes 262160 | tf_op jit(solution)/shard_map/reduce_scatter | solution.py:156
  533.3 17.8 %all-gather.41.cloned.1.call-done = bf16[512,1024]{1,0:T(8,128)(2,1)} async-done(((bf16[128,1024]{1,0:T(8,128)(2,1)}), bf16[512,1024]{1,0:T(8,128)(2,1)}) %all-gather.41.cloned.1.call-update) | async-done | bytes 1048592 | tf_op jit(solution)/shard_map/all_gather | solution.py:149
  580.8 26.8 %reduce-scatter.53.cloned.1.call-done = bf16[128,1024]{1,0:T(8,128)(2,1)} async-done(((bf16[512,1024]{1,0:T(8,128)(2,1)}), bf16[128,1024]{1,0:T(8,128)(2,1)}) %reduce-scatter.53.cloned.1.call-update) | async-done | bytes 262160 | tf_op jit(solution)/shard_map/reduce_scatter | solution.py:168
  610.8 26.6 %all-gather.43.cloned.1.call-done = bf16[512,1024]{1,0:T(8,128)(2,1)} async-done(((bf16[128,1024]{1,0:T(8,128)(2,1)}), bf16[512,1024]{1,0:T(8,128)(2,1)}) %all-gather.43.cloned.1.call-update) | async-done | bytes 1048592 | tf_op jit(solution)/shard_map/all_gather | solution.py:149
  644.8 26.8 %reduce-scatter.55.cloned.1.call-done = bf16[128,1024]{1,0:T(8,128)(2,1)} async-done(((bf16[512,1024]{1,0:T(8,128)(2,1)}), bf16[128,1024]{1,0:T(8,128)(2,1)}) %reduce-scatter.55.cloned.1.call-update) | async-done | bytes 262160 | tf_op jit(solution)/shard_map/reduce_scatter | solution.py:168
  675.0 26.4 %all-gather.45.cloned.1.call-done = bf16[512,1024]{1,0:T(8,128)(2,1)} async-done(((bf16[128,1024]{1,0:T(8,128)(2,1)}), bf16[512,1024]{1,0:T(8,128)(2,1)}) %all-gather.45.cloned.1.call-update) | async-done | bytes 1048592 | tf_op jit(solution)/shard_map/all_gather | solution.py:149
  778.5 21.3 %reduce-scatter.77.cloned.1.call-done = bf16[128,1024]{1,0:T(8,128)(2,1)} async-done(((bf16[1024,1024]{1,0:T(8,128)(2,1)}), bf16[128,1024]{1,0:T(8,128)(2,1)}) %reduce-scatter.77.cloned.1.call-update) | async-done | bytes 262160
  801.0 35.3 %reduce-scatter.69.cloned.1.call-done = bf16[32,2]{1,0:T(8,128)(2,1)} async-done(((bf16[256,2]{1,0:T(8,128)(2,1)}), bf16[32,2]{1,0:T(8,128)(2,1)}) %reduce-scatter.69.cloned.1.call-update) | async-done | bytes 144
  837.0 37.0 %reduce-scatter.73.cloned.1.call-done = bf16[128,256]{1,0:T(8,128)(2,1)} async-done(((bf16[1024,256]{1,0:T(8,128)(2,1)}), bf16[128,256]{1,0:T(8,128)(2,1)}) %reduce-scatter.73.cloned.1.call-update) | async-done | bytes 65552
  875.0 36.2 %reduce-scatter.81.cloned.1.call-done = bf16[128,2]{1,0:T(8,128)(2,1)} async-done(((bf16[1024,2]{1,0:T(8,128)(2,1)}), bf16[128,2]{1,0:T(8,128)(2,1)}) %reduce-scatter.81.cloned.1.call-update) | async-done | bytes 528
  912.0 35.7 %reduce-scatter.85.cloned.1.call-done = bf16[128,4]{1,0:T(8,128)(2,1)} async-done(((bf16[1024,4]{1,0:T(8,128)(2,1)}), bf16[128,4]{1,0:T(8,128)(2,1)}) %reduce-scatter.85.cloned.1.call-update) | async-done | bytes 1040
  961.5 30.7 %reduce-scatter.75.cloned.1.call-done = bf16[128,1024]{1,0:T(8,128)(2,1)} async-done(((bf16[1024,1024]{1,0:T(8,128)(2,1)}), bf16[128,1024]{1,0:T(8,128)(2,1)}) %reduce-scatter.75.cloned.1.call-update) | async-done | bytes 262160
  994.4 42.2 %reduce-scatter.65.cloned.1.call-done = bf16[128,1024]{1,0:T(8,128)(2,1)} async-done(((bf16[1024,1024]{1,0:T(8,128)(2,1)}), bf16[128,1024]{1,0:T(8,128)(2,1)}) %reduce-scatter.65.cloned.1.call-update) | async-done | bytes 262160 | tf_op jit(solution)/shard_map/reduce_scatter | solution.py:318
  1036.6 44.3 %reduce-scatter.63.cloned.1.call-done = bf16[128,1024]{1,0:T(8,128)(2,1)} async-done(((bf16[1024,1024]{1,0:T(8,128)(2,1)}), bf16[128,1024]{1,0:T(8,128)(2,1)}) %reduce-scatter.63.cloned.1.call-update) | async-done | bytes 262160 | tf_op jit(solution)/shard_map/reduce_scatter | solution.py:318
  1082.9 34.5 %reduce-scatter.67.cloned.1.call-done = bf16[32,2]{1,0:T(8,128)(2,1)} async-done(((bf16[256,2]{1,0:T(8,128)(2,1)}), bf16[32,2]{1,0:T(8,128)(2,1)}) %reduce-scatter.67.cloned.1.call-update) | async-done | bytes 144
  1118.8 35.9 %reduce-scatter.71.cloned.1.call-done = bf16[128,256]{1,0:T(8,128)(2,1)} async-done(((bf16[1024,256]{1,0:T(8,128)(2,1)}), bf16[128,256]{1,0:T(8,128)(2,1)}) %reduce-scatter.71.cloned.1.call-update) | async-done | bytes 65552
  1157.4 33.8 %reduce-scatter.79.cloned.1.call-done = bf16[128,2]{1,0:T(8,128)(2,1)} async-done(((bf16[1024,2]{1,0:T(8,128)(2,1)}), bf16[128,2]{1,0:T(8,128)(2,1)}) %reduce-scatter.79.cloned.1.call-update) | async-done | bytes 528
  1192.1 35.9 %reduce-scatter.83.cloned.1.call-done = bf16[128,4]{1,0:T(8,128)(2,1)} async-done(((bf16[1024,4]{1,0:T(8,128)(2,1)}), bf16[128,4]{1,0:T(8,128)(2,1)}) %reduce-scatter.83.cloned.1.call-update) | async-done | bytes 1040
  1241.3 28.4 %reduce-scatter.61.cloned.1.call-done = bf16[128,3,256]{2,0,1:T(8,128)(2,1)} async-done(((bf16[1024,3,256]{2,0,1:T(8,128)(2,1)}), bf16[128,3,256]{2,0,1:T(8,128)(2,1)}) %reduce-scatter.61.cloned.1.call-update) | async-done | bytes 196624 | tf_op jit(solution)/shard_map/reduce_scatter | solution.py:312
  1269.7 41.5 %reduce-scatter.59.cloned.1.call-done = bf16[128,3,256]{2,0,1:T(8,128)(2,1)} async-done(((bf16[1024,3,256]{2,0,1:T(8,128)(2,1)}), bf16[128,3,256]{2,0,1:T(8,128)(2,1)}) %reduce-scatter.59.cloned.1.call-update) | async-done | bytes 196624 | tf_op jit(solution)/shard_map/reduce_scatter | solution.py:312
  (359 shorter events, 353.9 us)
Async XLA Ops:
  32.3 56.0 %all-gather.47.cloned.1.call-start = ((), (), s32[]{:S(2)}) async-start(), calls=%async_computation.42 | async-start | bytes 1769472 | tf_op jit(solution)/shard_map/all_gather | solution.py:135
  33.2 91.8 %reduce-scatter.43.cloned.1.call-start = ((), (), s32[]{:S(2)}) async-start(), calls=%async_computation.23 | async-start | bytes 1310720 | tf_op jit(solution)/shard_map/reduce_scatter | solution.py:156
  97.5 56.1 %all-gather.49.cloned.1.call-start = ((), (), s32[]{:S(2)}) async-start(), calls=%async_computation.43 | async-start | bytes 2359296 | tf_op jit(solution)/shard_map/all_gather | solution.py:137
  98.4 85.2 %all-gather.33.cloned.1.call-start = ((), (), s32[]{:S(2)}) async-start(), calls=%async_computation.24 | async-start | bytes 1310720 | tf_op jit(solution)/shard_map/all_gather | solution.py:146
  127.2 86.2 %all-gather.51.cloned.1.call-start = ((), (), s32[]{:S(2)}) async-start(), calls=%async_computation.44 | async-start | bytes 2359296 | tf_op jit(solution)/shard_map/all_gather | solution.py:138
  128.1 117.5 %reduce-scatter.45.cloned.1.call-start = ((), (), s32[]{:S(2)}) async-start(), calls=%async_computation.25 | async-start | bytes 1310720 | tf_op jit(solution)/shard_map/reduce_scatter | solution.py:156
  219.0 84.2 %all-gather.35.cloned.1.call-start = ((), (), s32[]{:S(2)}) async-start(), calls=%async_computation.26 | async-start | bytes 1310720 | tf_op jit(solution)/shard_map/all_gather | solution.py:146
  247.8 91.5 %reduce-scatter.47.cloned.1.call-start = ((), (), s32[]{:S(2)}) async-start(), calls=%async_computation.27 | async-start | bytes 1310720 | tf_op jit(solution)/shard_map/reduce_scatter | solution.py:156
  313.2 84.9 %all-gather.37.cloned.1.call-start = ((), (), s32[]{:S(2)}) async-start(), calls=%async_computation.28 | async-start | bytes 1310720 | tf_op jit(solution)/shard_map/all_gather | solution.py:146
  341.5 86.1 %all-gather.39.cloned.1.call-start = ((), (), s32[]{:S(2)}) async-start(), calls=%async_computation.30 | async-start | bytes 1310720 | tf_op jit(solution)/shard_map/all_gather | solution.py:149
  342.3 115.1 %all-gather.57.cloned.1.call-start = ((), (), s32[]{:S(2)}) async-start(), calls=%async_computation.47 | async-start | bytes 2359296 | tf_op jit(solution)/shard_map/all_gather | solution.py:138
  342.9 150.2 %reduce-scatter.51.cloned.1.call-start = ((), (), s32[]{:S(2)}) async-start(), calls=%async_computation.31 | async-start | bytes 1310720 | tf_op jit(solution)/shard_map/reduce_scatter | solution.py:168
  470.4 80.7 %all-gather.41.cloned.1.call-start = ((), (), s32[]{:S(2)}) async-start(), calls=%async_computation.32 | async-start | bytes 1310720 | tf_op jit(solution)/shard_map/all_gather | solution.py:149
  524.5 83.1 %reduce-scatter.53.cloned.1.call-start = ((), (), s32[]{:S(2)}) async-start(), calls=%async_computation.33 | async-start | bytes 1310720 | tf_op jit(solution)/shard_map/reduce_scatter | solution.py:168
  580.8 56.7 %all-gather.43.cloned.1.call-start = ((), (), s32[]{:S(2)}) async-start(), calls=%async_computation.34 | async-start | bytes 1310720 | tf_op jit(solution)/shard_map/all_gather | solution.py:149
  610.8 60.7 %reduce-scatter.55.cloned.1.call-start = ((), (), s32[]{:S(2)}) async-start(), calls=%async_computation.35 | async-start | bytes 1310720 | tf_op jit(solution)/shard_map/reduce_scatter | solution.py:168
  644.7 56.6 %all-gather.45.cloned.1.call-start = ((), (), s32[]{:S(2)}) async-start(), calls=%async_computation.36 | async-start | bytes 1310720 | tf_op jit(solution)/shard_map/all_gather | solution.py:149
  674.7 91.1 %reduce-scatter.57.cloned.1.call-start = ((), (), s32[]{:S(2)}) async-start(), calls=%async_computation.37 | async-start | bytes 1310720 | tf_op jit(solution)/shard_map/reduce_scatter | solution.py:168
  730.1 69.7 %reduce-scatter.77.cloned.1.call-start = ((), (), s32[]{:S(2)}) async-start(), calls=%async_computation.53 | async-start | bytes 2359296
  738.9 97.4 %reduce-scatter.69.cloned.1.call-start = ((), (), s32[]{:S(2)}) async-start(), calls=%async_computation.49 | async-start | bytes 73728
  739.9 134.2 %reduce-scatter.73.cloned.1.call-start = ((), (), s32[]{:S(2)}) async-start(), calls=%async_computation.51 | async-start | bytes 589824
  741.6 169.6 %reduce-scatter.81.cloned.1.call-start = ((), (), s32[]{:S(2)}) async-start(), calls=%async_computation.55 | async-start | bytes 294912
  742.8 205.0 %reduce-scatter.85.cloned.1.call-start = ((), (), s32[]{:S(2)}) async-start(), calls=%async_computation.57 | async-start | bytes 294912
  743.8 248.4 %reduce-scatter.75.cloned.1.call-start = ((), (), s32[]{:S(2)}) async-start(), calls=%async_computation.52 | async-start | bytes 2359296
  752.7 283.9 %reduce-scatter.65.cloned.1.call-start = ((), (), s32[]{:S(2)}) async-start(), calls=%async_computation.41 | async-start | bytes 2359296 | tf_op jit(solution)/shard_map/reduce_scatter | solution.py:318
  757.8 323.1 %reduce-scatter.63.cloned.1.call-start = ((), (), s32[]{:S(2)}) async-start(), calls=%async_computation.40 | async-start | bytes 2359296 | tf_op jit(solution)/shard_map/reduce_scatter | solution.py:318
  762.9 354.6 %reduce-scatter.67.cloned.1.call-start = ((), (), s32[]{:S(2)}) async-start(), calls=%async_computation.48 | async-start | bytes 73728
  763.9 390.8 %reduce-scatter.71.cloned.1.call-start = ((), (), s32[]{:S(2)}) async-start(), calls=%async_computation.50 | async-start | bytes 589824
  765.6 425.6 %reduce-scatter.79.cloned.1.call-start = ((), (), s32[]{:S(2)}) async-start(), calls=%async_computation.54 | async-start | bytes 294912
  769.0 459.0 %reduce-scatter.83.cloned.1.call-start = ((), (), s32[]{:S(2)}) async-start(), calls=%async_computation.56 | async-start | bytes 294912
  770.1 499.6 %reduce-scatter.61.cloned.1.call-start = ((), (), s32[]{:S(2)}) async-start(), calls=%async_computation.39 | async-start | bytes 1769472 | tf_op jit(solution)/shard_map/reduce_scatter | solution.py:312
  773.7 537.4 %reduce-scatter.59.cloned.1.call-start = ((), (), s32[]{:S(2)}) async-start(), calls=%async_computation.38 | async-start | bytes 1769472 | tf_op jit(solution)/shard_map/reduce_scatter | solution.py:312
  (54 other events, 841.8 us)
Sparse Core Ops, SparseCore 0:
  32.4 28.2 all-gather.30
  97.6 27.2 reduce-scatter.42
  155.6 27.9 all-gather.32
  185.9 27.4 all-gather.50
  218.2 27.2 reduce-scatter.44
  275.8 27.3 all-gather.34
  312.6 26.6 reduce-scatter.46
  341.7 26.2 all-gather.54
  370.1 27.9 all-gather.36
  400.2 27.3 all-gather.38
  429.9 27.4 all-gather.56
  465.8 27.2 reduce-scatter.50
  524.6 26.4 all-gather.40
  580.9 26.6 reduce-scatter.52
  610.9 26.4 all-gather.42
  644.8 26.6 reduce-scatter.54
  674.9 26.4 all-gather.44
  730.2 26.6 reduce-scatter.56
  760.2 39.5 reduce-scatter.76
  802.7 33.5 reduce-scatter.68
  839.9 34.1 reduce-scatter.72
  877.5 33.6 reduce-scatter.80
  914.1 33.6 reduce-scatter.84
  951.1 41.0 reduce-scatter.74
  995.5 41.0 reduce-scatter.64
  1039.7 41.0 reduce-scatter.62
  1083.9 33.5 reduce-scatter.66
  1120.5 34.1 reduce-scatter.70
  1157.6 33.6 reduce-scatter.78
  1194.3 33.6 reduce-scatter.82
  1231.3 38.3 reduce-scatter.60
  1272.8 38.3 reduce-scatter.58
  (4 shorter events, 102.6 us)
where the time goes:
time: 1330 us; the launch traced here: 1320 us
  waiting for transfers between devices  967 us (73%)
  matrix products  127 us (10%)
  blocking collectives  118 us (9%)
  local copies, waits for them, and re-layouts  46.9 us (4%)
  other arithmetic  35.4 us (3%)
  between operations  16.3 us (1%)
    unnamed x46, waiting for transfers between devices  338 us
    all_gather x4, waiting for transfers between devices, collect_grad(): return lax.all_gather(own_part, 'tensor', axis=0, tiled=True)  95.8 us
    all_gather x4, waiting for transfers between devices, collect(): return lax.all_gather(own_part, 'tensor', axis=0, tiled=True)  94.3 us
    reduce_scatter x4, waiting for transfers between devices, reduce_rows(): lax.psum_scatter(term(jnp.int32(0), own_rows * lax.axis_size('tensor')).a...  89.3 us
    reduce_scatter x2, waiting for transfers between devices, shards(): lax.psum_scatter(layer_terms[2].astype(jnp.bfloat16), 'dp', scatter_dimen...  86.5 us
    reduce_scatter x4, waiting for transfers between devices, reduce_back(): lax.psum_scatter(term(jnp.int32(0), own_rows * lax.axis_size('tensor')).a...  76.2 us
    reduce_scatter x2, waiting for transfers between devices, shards(): lax.psum_scatter(layer_terms[0].astype(jnp.bfloat16), 'dp', scatter_dimen...  69.9 us
    all_gather x2, waiting for transfers between devices, fetch(): lax.all_gather(w_2[layer_index], 'dp', axis=1, tiled=True)  55.1 us
  transfers between devices with their start and end apart: 36, of which 35 were waited for; matrix products, arithmetic and copies ran while one was open for 7% of the time, Pallas kernels for 0%

commit v1 on v0

v1 whole, which is shorter than its diff:
```python
import math

import jax
import jax.numpy as jnp
from jax import lax
from jax.experimental import pallas as pl
from jax.experimental.pallas import tpu as pltpu
from jax.sharding import PartitionSpec as P

HEAD_DIM = 64


NORM_EPS = 1e-05
GELU_COEFF = 0.7978845608028654
GELU_CUBIC = 0.044715


def layer_norm(inputs, gain_row, bias_row):
    row_mean = jnp.mean(inputs, axis=-1, keepdims=True)
    centered = inputs - row_mean
    inv_std = lax.rsqrt(jnp.mean(centered * centered, axis=-1, keepdims=True) + NORM_EPS)
    normed = centered * inv_std
    return (normed * gain_row + bias_row, normed, inv_std)


def norm_back(grad_in, normed, inv_std, gain_row):
    scaled = grad_in * gain_row
    return inv_std * (
        scaled
        - jnp.mean(scaled, axis=-1, keepdims=True)
        - normed * jnp.mean(scaled * normed, axis=-1, keepdims=True)
    )


def gelu_pair(pre_act):
    squared = pre_act * pre_act
    tangent = jnp.tanh(GELU_COEFF * (pre_act + GELU_CUBIC * squared * pre_act))
    gelu_value = 0.5 * pre_act * (1.0 + tangent)
    gelu_slope = 0.5 * (1.0 + tangent) + 0.5 * pre_act * (1.0 - tangent * tangent) * GELU_COEFF * (
        1.0 + 3.0 * GELU_CUBIC * squared
    )
    return (gelu_value, gelu_slope)


def segment_ids(lengths, total_rows):
    sequence_ends = jnp.cumsum(lengths)
    positions = jnp.arange(total_rows, dtype=jnp.int32)
    return jnp.sum(
        (positions[:, None] >= sequence_ends[None, :]).astype(jnp.int32), axis=1, dtype=jnp.int32
    )


def contract_first(left, right):
    return lax.dot_general(
        left, right, (((0,), (0,)), ((), ())), preferred_element_type=jnp.float32
    )


def contract_last(left, right):
    return lax.dot_general(
        left, right, (((1,), (1,)), ((), ())), preferred_element_type=jnp.float32
    )

def exchange_kernel(plan, *refs):
    count = len(plan)
    ins = refs[:count]
    outs = refs[count : 2 * count]
    send_sem, recv_sem, own_sem = refs[2 * count :]

    greeted = []
    for axis in sorted({axis for axis, _, _ in plan}):
        kinds = {kind for name, kind, _ in plan if name == axis}
        size = [n for name, _, n in plan if name == axis][0]
        me = lax.axis_index(axis)
        if kinds == {"paired"}:
            greeted.append({axis: me + 1 - 2 * (me % 2)})
            greeted += [{axis: (me + k) % size} for k in range(2, size, 2)]
        else:
            greeted += [{axis: (me + k) % size} for k in range(1, size)]
    barrier = pltpu.get_barrier_semaphore()
    for device in greeted:
        pl.semaphore_signal(
            barrier, inc=1, device_id=device, device_id_type=pl.DeviceIdType.MESH
        )
    pl.semaphore_wait(barrier, len(greeted))

    used = [0]

    def remote(src, dst, device):
        slot = used[0]
        used[0] += 1
        copy = pltpu.make_async_remote_copy(
            src_ref=src,
            dst_ref=dst,
            send_sem=send_sem.at[slot],
            recv_sem=recv_sem.at[slot],
            device_id=device,
            device_id_type=pl.DeviceIdType.MESH,
        )
        copy.start()
        return copy

    started = []
    relays = []
    own = []
    for index, (axis, kind, size) in enumerate(plan):
        me = lax.axis_index(axis)
        src, dst = ins[index], outs[index]
        if kind == "paired":
            for k in range(2, size, 2):
                copy = remote(src, dst.at[me], {axis: (me + k) % size})
                relays.append((copy, dst, axis, (me + size - k) % size))
            started.append(remote(src, dst.at[me], {axis: me + 1 - 2 * (me % 2)}))
        else:
            for k in range(1, size):
                peer = (me + k) % size
                block = src if kind == "gather" else src.at[peer]
                started.append(remote(block, dst.at[me], {axis: peer}))
    for index, (axis, kind, size) in enumerate(plan):
        me = lax.axis_index(axis)
        block = ins[index].at[me] if kind == "swap" else ins[index]
        copy = pltpu.make_async_copy(block, outs[index].at[me], own_sem.at[index])
        copy.start()
        own.append(copy)
    for copy, dst, axis, slot in relays:
        copy.wait_recv()
        me = lax.axis_index(axis)
        started.append(
            remote(dst.at[slot], dst.at[slot], {axis: me + 1 - 2 * (me % 2)})
        )
    for copy, _, _, _ in relays:
        copy.wait_send()
    for copy in own:
        copy.wait()
    for copy in started:
        copy.wait()


def make_exchange():
    calls = [0]

    def exchange(*items):
        plan = []
        shapes = []
        copies = 0
        sent = 0
        for axis, kind, value in items:
            size = lax.axis_size(axis)
            if kind == "paired" and size % 2:
                kind = "gather"
            plan.append((axis, kind, size))
            copies += size - 1
            block = value.shape[1:] if kind == "swap" else value.shape
            shapes.append(jax.ShapeDtypeStruct((size,) + block, value.dtype))
            sent += (size - 1) * math.prod(block) * value.dtype.itemsize
        collective_id = calls[0]
        calls[0] += 1
        return pl.pallas_call(
            lambda *refs: exchange_kernel(tuple(plan), *refs),
            out_shape=tuple(shapes),
            in_specs=[pl.BlockSpec(memory_space=pltpu.VMEM)] * len(plan),
            out_specs=tuple([pl.BlockSpec(memory_space=pltpu.VMEM)] * len(plan)),
            scratch_shapes=[
                pltpu.SemaphoreType.DMA((copies,)),
                pltpu.SemaphoreType.DMA((copies,)),
                pltpu.SemaphoreType.DMA((len(plan),)),
            ],
            compiler_params=pltpu.CompilerParams(
                collective_id=collective_id,
                has_side_effects=True,
                vmem_limit_bytes=48 * 1024 * 1024,
            ),
            cost_estimate=pl.CostEstimate(flops=0, bytes_accessed=sent, transcendentals=0),
            name=f"exchange_{collective_id}",
        )(*[value for _, _, value in items])

    return exchange


def masked_scores(queries, key_vecs, segments, score_scale):
    positions = jnp.arange(key_vecs.shape[0], dtype=jnp.int32)
    allowed = (segments[:, None] == segments[None, :]) & (
        positions[None, :] <= positions[:, None]
    )
    scores = (
        jnp.einsum("qhd,khd->hqk", queries, key_vecs, preferred_element_type=jnp.float32)
        * score_scale
    )
    return jnp.where(allowed[None], scores, -jnp.inf)


def attend(queries, key_vecs, val_vecs, segments, score_scale):
    scores = masked_scores(queries, key_vecs, segments, score_scale)
    row_max = jnp.max(scores, axis=-1, keepdims=True)
    log_total = row_max + jnp.log(jnp.sum(jnp.exp(scores - row_max), axis=-1, keepdims=True))
    probs_half = jnp.exp(scores - log_total).astype(jnp.bfloat16)
    attended = jnp.einsum("hqk,khd->qhd", probs_half, val_vecs, preferred_element_type=jnp.float32)
    return (attended.astype(jnp.bfloat16).reshape(queries.shape[0], -1), log_total)


def attend_back(queries, key_vecs, val_vecs, grad_attended, log_total, segments, score_scale):
    scores = masked_scores(queries, key_vecs, segments, score_scale)
    soft_probs = jnp.exp(scores - log_total)
    probs_half = soft_probs.astype(jnp.bfloat16)
    grad_probs = jnp.einsum(
        "qhd,khd->hqk", grad_attended, val_vecs, preferred_element_type=jnp.float32
    )
    val_grad = jnp.einsum(
        "hqk,qhd->khd", probs_half, grad_attended, preferred_element_type=jnp.float32
    )
    row_dot = jnp.sum(grad_probs * soft_probs, axis=-1, keepdims=True)
    score_grad = (soft_probs * (grad_probs - row_dot) * score_scale).astype(jnp.bfloat16)
    query_grad = jnp.einsum(
        "hqk,khd->qhd", score_grad, key_vecs, preferred_element_type=jnp.float32
    )
    key_grad = jnp.einsum("hqk,qhd->khd", score_grad, queries, preferred_element_type=jnp.float32)
    return (query_grad, key_grad, val_grad)


def pack(pieces, width, tile):
    flat = jnp.concatenate([piece.reshape(-1) for piece in pieces])
    unit = width * tile
    return jnp.pad(flat, (0, -flat.shape[0] % unit)).reshape(-1, width)


def unpack(packed, shapes):
    flat = packed.reshape(packed.shape[0], -1)
    pieces = []
    at = 0
    for shape in shapes:
        length = math.prod(shape)
        pieces.append(flat[:, at : at + length].reshape((packed.shape[0],) + shape))
        at += length
    return pieces


def shards(x_in, d_out, seq_lengths, w_qkv, b_qv, w_o, w_1, b_ffn, w_2, norm_gains, vec_biases):
    exchange = make_exchange()
    own_rows, width = x_in.shape
    tensor_size = lax.axis_size("tensor")
    dp_size = lax.axis_size("dp")
    group_rows = own_rows * tensor_size
    layer_count = w_qkv.shape[0]
    local_width = w_qkv.shape[3]
    local_heads = local_width // HEAD_DIM
    qkv_width = 3 * local_width
    score_scale = 1.0 / math.sqrt(HEAD_DIM)
    segments = segment_ids(seq_lengths[0], group_rows)
    half = jnp.bfloat16

    def shard_of(name, layer_index):
        if name == "qkv":
            return w_qkv[layer_index].reshape(w_qkv.shape[1], qkv_width)
        if name == "out":
            return w_o[layer_index].T
        if name == "up":
            return w_1[layer_index]
        return w_2[layer_index].T

    weights = {}

    def step(tensor_items, fetched=(), sums=()):
        items = [("tensor", kind, value) for kind, value in tensor_items]
        items += [("dp", "paired", shard_of(*key)) for key in fetched]
        items += [("dp", "swap", value) for value in sums]
        results = list(exchange(*items))
        for position, key in enumerate(fetched):
            piece = results[len(tensor_items) + position]
            weights[key] = piece.reshape(dp_size * piece.shape[1], piece.shape[2])
        gathered = [
            piece.reshape(group_rows, width) if kind == "gather" else piece.astype(jnp.float32).sum(0)
            for (kind, _), piece in zip(tensor_items, results)
        ]
        totals = [
            piece.astype(jnp.float32).sum(0) for piece in results[len(items) - len(sums) :]
        ]
        return gathered, totals

    def to_owners(partial):
        return ("swap", partial.astype(half).reshape(tensor_size, own_rows, width))

    def by_owner(gradient):
        return gradient.astype(half).reshape(dp_size, -1, gradient.shape[-1])

    small_shapes = [b_qv.shape, b_ffn.shape, norm_gains.shape, vec_biases.shape]
    small = pack([b_qv, b_ffn, norm_gains, vec_biases], 128, 16)
    first = exchange(
        ("tensor", "gather", d_out.astype(half)),
        ("dp", "paired", small),
        ("dp", "paired", shard_of("qkv", 0)),
    )
    last_grad_half = first[0].reshape(group_rows, width)
    weights["qkv", 0] = first[2].reshape(width, qkv_width)
    qv_all, ffn_all, gain_all, bias_all = [
        jnp.moveaxis(piece, 0, -2).reshape(piece.shape[1:-1] + (-1,)).astype(jnp.float32)
        for piece in unpack(first[1], small_shapes)
    ]

    caches = []
    hidden_in = x_in
    for layer_index in range(layer_count):
        last = layer_index == layer_count - 1
        following = layer_index + 1
        gain_rows = gain_all[layer_index]
        bias_rows = bias_all[layer_index]
        normed_own, unit_one, inv_one = layer_norm(hidden_in, gain_rows[0], bias_rows[0])
        fetched = [("out", 0), ("up", 0)] if layer_index == 0 else [("down", layer_index)]
        (normed_one,), _ = step([("gather", normed_own.astype(half))], fetched)
        projected = jnp.dot(
            normed_one, weights["qkv", layer_index], preferred_element_type=jnp.float32
        ).reshape(group_rows, 3, local_width)
        qv_bias = qv_all[layer_index]
        heads = (group_rows, local_heads, HEAD_DIM)
        queries = (projected[:, 0] + qv_bias[0]).astype(half).reshape(heads)
        key_vecs = projected[:, 1].astype(half).reshape(heads)
        val_vecs = (projected[:, 2] + qv_bias[1]).astype(half).reshape(heads)
        attended, log_total = attend(queries, key_vecs, val_vecs, segments, score_scale)
        fetched = [("down", 0)] if layer_index == 0 else []
        (summed,), _ = step(
            [to_owners(contract_last(attended, weights["out", layer_index]))], fetched
        )
        residual_mid = hidden_in + summed + bias_rows[2]
        normed_own_two, unit_two, inv_two = layer_norm(residual_mid, gain_rows[1], bias_rows[1])
        fetched = [] if last else [("qkv", following), ("out", following)]
        (normed_two,), _ = step([("gather", normed_own_two.astype(half))], fetched)
        pre_act = (
            jnp.dot(normed_two, weights["up", layer_index], preferred_element_type=jnp.float32)
            + ffn_all[layer_index]
        )
        gelu_value, gelu_slope = gelu_pair(pre_act)
        activated = gelu_value.astype(half)
        ffn_partial = to_owners(contract_last(activated, weights["down", layer_index]))
        if not last:
            (summed,), _ = step([ffn_partial], [("up", following)])
            hidden_in = residual_mid + summed + bias_rows[3]
        caches.append(
            (
                unit_one,
                inv_one,
                normed_one,
                queries,
                key_vecs,
                val_vecs,
                attended,
                log_total,
                unit_two,
                inv_two,
                normed_two,
                activated,
                gelu_slope,
            )
        )
    back = d_out
    grads = {}
    small_terms = [None] * layer_count
    output = None
    for layer_index in reversed(range(layer_count)):
        last = layer_index == layer_count - 1
        gain_rows = gain_all[layer_index]
        (
            unit_one,
            inv_one,
            normed_one,
            queries,
            key_vecs,
            val_vecs,
            attended,
            log_total,
            unit_two,
            inv_two,
            normed_two,
            activated,
            gelu_slope,
        ) = caches[layer_index]
        if last:
            grad_half = last_grad_half
        else:
            (grad_half,), _ = step([("gather", back.astype(half))])
        grad_down = by_owner(contract_first(grad_half, activated))
        grad_pre = (
            jnp.dot(grad_half, weights["down", layer_index], preferred_element_type=jnp.float32)
            * gelu_slope
        )
        grad_pre_half = grad_pre.astype(half)
        grad_up = by_owner(contract_first(normed_two, grad_pre_half))
        partial = to_owners(contract_last(grad_pre_half, weights["up", layer_index]))
        if last:
            (grad_normed_two, summed), (grads["down", layer_index],) = step(
                [partial, ffn_partial], sums=[grad_down]
            )
            output = residual_mid + summed + bias_all[layer_index][3]
        else:
            (grad_normed_two,), (grads["down", layer_index],) = step([partial], sums=[grad_down])
        grad_mid = back + norm_back(grad_normed_two, unit_two, inv_two, gain_rows[1])
        (grad_mid_half,), (grads["up", layer_index],) = step(
            [("gather", grad_mid.astype(half))], sums=[grad_up]
        )
        grad_out = by_owner(contract_first(grad_mid_half, attended))
        grad_attended = jnp.dot(
            grad_mid_half, weights["out", layer_index], preferred_element_type=jnp.float32
        )
        grad_attended = grad_attended.astype(half).reshape(group_rows, local_heads, HEAD_DIM)
        query_grad, key_grad, val_grad = attend_back(
            queries, key_vecs, val_vecs, grad_attended, log_total, segments, score_scale
        )
        flat = (group_rows, local_width)
        grad_qkv = jnp.concatenate(
            [part.astype(half).reshape(flat) for part in (query_grad, key_grad, val_grad)], axis=1
        )
        grad_qkv_weight = by_owner(contract_first(normed_one, grad_qkv))
        (grad_normed_one,), (grads["qkv", layer_index], grads["out", layer_index]) = step(
            [to_owners(contract_last(grad_qkv, weights["qkv", layer_index]))],
            sums=[grad_qkv_weight, grad_out],
        )
        small_terms[layer_index] = (
            jnp.stack(
                [
                    jnp.sum(query_grad, axis=0).reshape(local_width),
                    jnp.sum(val_grad, axis=0).reshape(local_width),
                ]
            ),
            jnp.sum(grad_pre, axis=0),
            jnp.stack(
                [
                    jnp.sum(grad_normed_one * unit_one, axis=0),
                    jnp.sum(grad_normed_two * unit_two, axis=0),
                ]
            ),
            jnp.stack(
                [
                    jnp.sum(grad_normed_one, axis=0),
                    jnp.sum(grad_normed_two, axis=0),
                    jnp.sum(grad_mid, axis=0),
                    jnp.sum(back, axis=0),
                ]
            ),
        )
        back = grad_mid + norm_back(grad_normed_one, unit_one, inv_one, gain_rows[0])

    def split_owner(piece):
        return jnp.moveaxis(
            piece.reshape(piece.shape[:-1] + (dp_size, -1)), -2, 0
        ).reshape(dp_size, -1)

    stacked = [
        split_owner(jnp.stack([small_terms[index][member] for index in range(layer_count)]))
        for member in (2, 3, 0, 1)
    ]
    flat = jnp.concatenate(stacked, axis=1)
    flat = jnp.pad(flat, ((0, 0), (0, -flat.shape[1] % 1024)))
    (parts,) = exchange(("dp", "swap", flat.reshape(dp_size, -1, 128)))
    total = parts.sum(0)
    (shared,) = exchange(("tensor", "gather", total))
    everyone = shared.sum(0).reshape(-1)
    gain_size, bias_size = norm_gains.size, vec_biases.size
    mine = total.reshape(-1)[gain_size + bias_size :]

    def stack_layers(name, shape, transposed):
        parts = [grads[name, index] for index in range(layer_count)]
        return jnp.stack([part.T if transposed else part for part in parts]).reshape(shape)

    return (
        output,
        back,
        stack_layers("qkv", w_qkv.shape, False),
        mine[: b_qv.size].reshape(b_qv.shape),
        stack_layers("out", w_o.shape, True),
        stack_layers("up", w_1.shape, False),
        mine[b_qv.size : b_qv.size + b_ffn.size].reshape(b_ffn.shape),
        stack_layers("down", w_2.shape, True),
        everyone[:gain_size].reshape(norm_gains.shape),
        everyone[gain_size : gain_size + bias_size].reshape(vec_biases.shape),
    )


def solution(mesh):
    in_specs = (
        P(("dp", "tensor"), None),
        P(("dp", "tensor"), None),
        P("dp", None),
        P(None, "dp", None, "tensor"),
        P(None, None, ("tensor", "dp")),
        P(None, "tensor", "dp"),
        P(None, "dp", "tensor"),
        P(None, ("tensor", "dp")),
        P(None, "tensor", "dp"),
        P(None, None, "dp"),
        P(None, None, "dp"),
    )
    out_specs = (
        P(("dp", "tensor"), None),
        P(("dp", "tensor"), None),
        P(None, "dp", None, "tensor"),
        P(None, None, ("tensor", "dp")),
        P(None, "tensor", "dp"),
        P(None, "dp", "tensor"),
        P(None, ("tensor", "dp")),
        P(None, "tensor", "dp"),
        P(None, None, "dp"),
        P(None, None, "dp"),
    )
    return jax.shard_map(shards, mesh=mesh, in_specs=in_specs, out_specs=out_specs, check_vma=False)
```

time: 1330 us -> 588 us (0.44)
  waiting for transfers between devices: 967 us -> 0 us
  Pallas kernels: 0 us -> 426 us
  blocking collectives: 118 us -> 0 us
  matrix products: 127 us -> 91.7 us
  local copies, waits for them, and re-layouts: 46.9 us -> 24.7 us
  between operations: 16.3 us -> 2.8 us
    pallas_call x0 -> x17, Pallas kernels: none -> 426 us  [exchange(): pl.pallas_call(lambda *refs: exchange_kernel(tuple(plan), *refs), out_sha...]
    unnamed x46 -> x0, waiting for transfers between devices: 338 us -> none
    reduce_scatter x12 -> x0, waiting for transfers between devices: 322 us -> none  [the longest x4 89.3 us: reduce_rows(): lax.psum_scatter(term(jnp.int32(0), own_rows * lax.axis_size('tensor')).a...]
    all_gather x14 -> x0, waiting for transfers between devices: 307 us -> none  [the longest x4 95.8 us: collect_grad(): return lax.all_gather(own_part, 'tensor', axis=0, tiled=True)]
    all_gather x10 -> x0, blocking collectives: 92.9 us -> none  [the longest x2 21.9 us: fetch(): lax.all_gather(w_o[layer_index], 'dp', axis=1, tiled=True)]
    unnamed x125 -> x213, local copies, waits for them, and re-layouts: 35.5 us -> 11.6 us
    dot_general x8, matrix products: 24.9 us -> 10.8 us  [contract_last(): lax.dot_general(left, right, (((1,), (1,)), ((), ())), preferred_element_...]
  transfers between devices with their start and end apart: 36 -> 0, of which waited for: 35 -> 0; matrix products, arithmetic and copies ran while one was open for 7% -> 0% of each run, Pallas kernels for 0% -> 0%
where the time goes in v1:
time: 588 us; the launch traced here: 578 us
  Pallas kernels  426 us (72%)
  matrix products  91.7 us (16%)
  other arithmetic  33.4 us (6%)
  local copies, waits for them, and re-layouts  24.7 us (4%)
    pallas_call x17, Pallas kernels, exchange(): pl.pallas_call(lambda *refs: exchange_kernel(tuple(plan), *refs), out_sha...  426 us
    dot_general x2, matrix products, attend_back(): jnp.einsum('hqk,khd->qhd', score_grad, key_vecs, preferred_element_type=j...  19.5 us
    dot_general x2, matrix products, attend_back(): jnp.einsum('hqk,qhd->khd', score_grad, queries, preferred_element_type=jn...  15.8 us
    dot_general x8, matrix products, contract_first(): lax.dot_general(left, right, (((0,), (0,)), ((), ())), preferred_element_...  14.8 us

profile of v1, /device:TPU:0, one launch (start us, length us, event | category | flops | bytes accessed | tf_op | source)
XLA Modules:
  0.0 578.4 jit_solution(3213275012992496828)
XLA Ops:
  9.4 25.3 %exchange_0.1 = (bf16[4,128,1024]{2,1,0:T(8,128)(2,1)S(1)}, bf16[8,16,128]{2,1,0:T(8,128)(2,1)S(1)}, bf16[8,128,768]{2,1,0:T(8,128)(2,1)S(1)}) custom-call(bf16[128,1024]{1,0:T(8,128)(2,1)S(1)} %get-tuple-element.151.refs_0_, bf16[16,128]{1,0:T(8,128)(2,1)S(1)} %fusion.64.refs_1_, bf16[128,768]{1,0:T(8,128)(2,1)S(1)} %copy.101.refs_2_), custom_call_target="tpu_custom_call" | custom-call | bytes 2191360 | tf_op jit(solution)/shard_map/exchange_0/pallas_call | solution.py:158
  39.2 25.4 %exchange_1.1 = (bf16[4,128,1024]{2,1,0:T(8,128)(2,1)S(1)}, bf16[8,128,256]{2,1,0:T(8,128)(2,1)S(1)}, bf16[8,128,1024]{2,1,0:T(8,128)(2,1)S(1)}) custom-call(bf16[128,1024]{1,0:T(8,128)(2,1)S(1)} %add_convert_fusion.7.refs_0_, bf16[128,256]{1,0:T(8,128)(2,1)S(1)} %bitcast.268, bf16[128,1024]{1,0:T(8,128)(2,1)S(1)} %get-tuple-element.164.refs_2_), custom_call_target="tpu_custom_call" | custom-call | bytes 3080192 | tf_op jit(solution)/shard_map/exchange_1/pallas_call | solution.py:158
  64.6 3.6 fusion.101
  73.8 25.4 %exchange_2.1 = (bf16[4,128,1024]{2,1,0:T(8,128)(2,1)S(1)}, bf16[8,128,1024]{2,1,0:T(8,128)(2,1)S(1)}) custom-call(bf16[4,128,1024]{2,1,0:T(8,128)(2,1)S(1)} %bitcast.242, bf16[128,1024]{1,0:T(8,128)(2,1)S(1)} %bitcast.264), custom_call_target="tpu_custom_call" | custom-call | bytes 2621440 | tf_op jit(solution)/shard_map/exchange_2/pallas_call | solution.py:158
  100.8 25.2 %exchange_3.1 = (bf16[4,128,1024]{2,1,0:T(8,128)(2,1)S(1)}, bf16[8,128,768]{2,1,0:T(8,128)(2,1)S(1)}, bf16[8,128,256]{2,1,0:T(8,128)(2,1)S(1)}) custom-call(bf16[128,1024]{1,0:T(8,128)(2,1)S(1)} %add_convert_fusion.4.refs_0_, bf16[128,768]{1,0:T(8,128)(2,1)S(1)} %copy.109.refs_1_, bf16[128,256]{1,0:T(8,128)(2,1)S(1)} %bitcast.270), custom_call_target="tpu_custom_call" | custom-call | bytes 2621440 | tf_op jit(solution)/shard_map/exchange_3/pallas_call | solution.py:158
  128.8 3.3 fusion.102
  133.6 24.7 %exchange_4.1 = (bf16[4,128,1024]{2,1,0:T(8,128)(2,1)S(1)}, bf16[8,128,1024]{2,1,0:T(8,128)(2,1)S(1)}) custom-call(bf16[4,128,1024]{2,1,0:T(8,128)(2,1)S(1)} %bitcast.263, bf16[128,1024]{1,0:T(8,128)(2,1)S(1)} %get-tuple-element.163.refs_1_), custom_call_target="tpu_custom_call" | custom-call | bytes 2621440 | tf_op jit(solution)/shard_map/exchange_4/pallas_call | solution.py:158
  159.1 23.8 %exchange_5.1 = (bf16[4,128,1024]{2,1,0:T(8,128)(2,1)S(1)}, bf16[8,128,1024]{2,1,0:T(8,128)(2,1)S(1)}) custom-call(bf16[128,1024]{1,0:T(8,128)(2,1)S(1)} %add_convert_fusion.3.refs_0_, bf16[128,1024]{1,0:T(8,128)(2,1)S(1)} %bitcast.265), custom_call_target="tpu_custom_call" | custom-call | bytes 2621440 | tf_op jit(solution)/shard_map/exchange_5/pallas_call | solution.py:158
  188.6 21.7 %exchange_6.1 = bf16[4,128,1024]{2,1,0:T(8,128)(2,1)S(1)} custom-call(bf16[4,128,1024]{2,1,0:T(8,128)(2,1)S(1)} %bitcast.243), custom_call_target="tpu_custom_call" | custom-call | bytes 786432 | tf_op jit(solution)/shard_map/exchange_6/pallas_call | solution.py:158
  211.1 26.1 %exchange_7.1 = bf16[4,128,1024]{2,1,0:T(8,128)(2,1)S(1)} custom-call(bf16[128,1024]{1,0:T(8,128)(2,1)S(1)} %add_convert_fusion.refs_0_), custom_call_target="tpu_custom_call" | custom-call | bytes 786432 | tf_op jit(solution)/shard_map/exchange_7/pallas_call | solution.py:158
  240.0 2.9 fusion.99
  242.8 2.8 convolution_convert_fusion.3
  246.9 50.0 %exchange_8.1 = (bf16[4,128,1024]{2,1,0:T(8,128)(2,1)S(1)}, bf16[4,128,1024]{2,1,0:T(8,128)(2,1)S(1)}, bf16[8,128,1024]{2,1,0:T(8,128)(2,1)}) custom-call(bf16[4,128,1024]{2,1,0:T(8,128)(2,1)S(1)} %bitcast.267, bf16[4,128,1024]{2,1,0:T(8,128)(2,1)S(1)} %bitcast.266, bf16[8,128,1024]{2,1,0:T(8,128)(2,1)} %bitcast.289), custom_call_target="tpu_custom_call" | custom-call | bytes 3407872 | tf_op jit(solution)/shard_map/exchange_8/pallas_call | solution.py:158
  303.0 28.8 %exchange_9.1 = (bf16[4,128,1024]{2,1,0:T(8,128)(2,1)S(1)}, bf16[8,128,1024]{2,1,0:T(8,128)(2,1)S(1)}) custom-call(bf16[128,1024]{1,0:T(8,128)(2,1)S(1)} %convert_element_type.314.refs_0_, bf16[8,128,1024]{2,1,0:T(8,128)(2,1)S(1)} %bitcast.248), custom_call_target="tpu_custom_call" | custom-call | bytes 2621440 | tf_op jit(solution)/shard_map/exchange_9/pallas_call | solution.py:158
  336.6 2.9 fusion.53
  339.5 8.1 %fusion.39 = bf16[4,64,512]{2,1,0:T(8,128)(2,1)} fusion(f32[4,512,512]{1,2,0:T(8,128)} %fusion.53, f32[512,4,64]{0,2,1:T(8,128)S(1)} %bitcast.297, f32[4,64]{1,0:T(4,128)S(1)} %add.281, f32[4,512,512]{1,2,0:T(8,128)} %copy-done.26, f32[4,512]{1,0:T(4,128)S(1)} %log_add_fusion, pred[512,512]{0,1:T(8,128)(4,1)S(1)} %copy-done.28), kind=kOutput, calls=%fused_computation.73 | convolution fusion | flops 146147840 | bytes 9446400 | tf_op jit(solution)/shard_map/hqk,qhd->khd/dot_general | solution.py:216
  347.7 9.5 %fusion.88 = (f32[4,64]{1,0:T(4,128)S(1)}, bf16[512,4,64]{0,2,1:T(8,128)(2,1)}) fusion(bf16[512,4,64]{0,2,1:T(8,128)(2,1)S(1)} %bitcast.319, f32[4,512,512]{1,2,0:T(8,128)} %fusion.53, f32[4,512]{1,0:T(4,128)S(1)} %log_add_fusion, f32[4,512,512]{1,2,0:T(8,128)} %copy-done.26, pred[512,512]{0,1:T(8,128)(4,1)S(1)} %copy-done.28), kind=kOutput, calls=%fused_computation.215 | convolution fusion | flops 146016512 | bytes 9184256 | tf_op jit(solution)/shard_map/hqk,khd->qhd/dot_general | solution.py:213
  359.4 2.2 convolution_convert_fusion.5
  361.6 30.4 %exchange_10.1 = (bf16[4,128,1024]{2,1,0:T(8,128)(2,1)S(1)}, bf16[8,128,768]{2,1,0:T(8,128)(2,1)S(1)}, bf16[8,128,256]{2,1,0:T(8,128)(2,1)S(1)}) custom-call(bf16[4,128,1024]{2,1,0:T(8,128)(2,1)S(1)} %bitcast.256, bf16[8,128,768]{2,1,0:T(8,128)(2,1)} %bitcast.303, bf16[8,128,256]{2,1,0:T(8,128)(2,1)S(1)} %bitcast.251), custom_call_target="tpu_custom_call" | custom-call | bytes 2621440 | tf_op jit(solution)/shard_map/exchange_10/pallas_call | solution.py:158
  401.8 21.4 %exchange_11.1 = bf16[4,128,1024]{2,1,0:T(8,128)(2,1)S(1)} custom-call(bf16[128,1024]{1,0:T(8,128)(2,1)S(1)} %convert_element_type.326.refs_0_), custom_call_target="tpu_custom_call" | custom-call | bytes 786432 | tf_op jit(solution)/shard_map/exchange_11/pallas_call | solution.py:158
  423.3 4.0 fusion.100
  427.3 2.8 convolution_convert_fusion.1
  431.4 30.7 %exchange_12.1 = (bf16[4,128,1024]{2,1,0:T(8,128)(2,1)S(1)}, bf16[8,128,1024]{2,1,0:T(8,128)(2,1)S(1)}) custom-call(bf16[4,128,1024]{2,1,0:T(8,128)(2,1)S(1)} %bitcast.258, bf16[8,128,1024]{2,1,0:T(8,128)(2,1)} %bitcast.288), custom_call_target="tpu_custom_call" | custom-call | bytes 2621440 | tf_op jit(solution)/shard_map/exchange_12/pallas_call | solution.py:158
  467.4 2.6 convolution_convert_fusion
  470.0 27.4 %exchange_13.1 = (bf16[4,128,1024]{2,1,0:T(8,128)(2,1)S(1)}, bf16[8,128,1024]{2,1,0:T(8,128)(2,1)S(1)}) custom-call(bf16[128,1024]{1,0:T(8,128)(2,1)S(1)} %convert_element_type.331.refs_0_, bf16[8,128,1024]{2,1,0:T(8,128)(2,1)S(1)} %bitcast.249), custom_call_target="tpu_custom_call" | custom-call | bytes 2621440 | tf_op jit(solution)/shard_map/exchange_13/pallas_call | solution.py:158
  503.5 2.9 fusion.51
  506.4 7.6 %fusion.36 = bf16[4,64,512]{2,1,0:T(8,128)(2,1)S(1)} fusion(f32[4,512,512]{1,2,0:T(8,128)} %fusion.51, f32[512,4,64]{0,2,1:T(8,128)S(1)} %bitcast.291, f32[4,64]{1,0:T(4,128)S(1)} %copy-done.77, f32[4,512,512]{1,2,0:T(8,128)} %copy-done.24, f32[4,512]{1,0:T(4,128)S(1)} %copy-done.82, pred[512,512]{0,1:T(8,128)(4,1)S(1)} %copy-done.28), kind=kOutput, calls=%fused_computation.72 | convolution fusion | flops 146147840 | bytes 9446400 | tf_op jit(solution)/shard_map/hqk,qhd->khd/dot_general | solution.py:216
  514.0 10.0 %fusion.86 = (f32[4,64]{1,0:T(4,128)}, bf16[512,4,64]{0,2,1:T(8,128)(2,1)}) fusion(bf16[512,4,64]{0,2,1:T(8,128)(2,1)S(1)} %bitcast.317, f32[4,512,512]{1,2,0:T(8,128)} %fusion.51, f32[4,512]{1,0:T(4,128)S(1)} %copy-done.82, f32[4,512,512]{1,2,0:T(8,128)} %copy-done.24, pred[512,512]{0,1:T(8,128)(4,1)S(1)} %copy-done.28), kind=kOutput, calls=%fused_computation.213 | convolution fusion | flops 146016512 | bytes 9184256 | tf_op jit(solution)/shard_map/hqk,khd->qhd/dot_general | solution.py:213
  526.2 2.2 convolution_convert_fusion.4
  528.5 29.0 %exchange_14.1 = (bf16[4,128,1024]{2,1,0:T(8,128)(2,1)S(1)}, bf16[8,128,768]{2,1,0:T(8,128)(2,1)S(1)}, bf16[8,128,256]{2,1,0:T(8,128)(2,1)S(1)}) custom-call(bf16[4,128,1024]{2,1,0:T(8,128)(2,1)S(1)} %bitcast.257, bf16[8,128,768]{2,1,0:T(8,128)(2,1)} %bitcast.304, bf16[8,128,256]{2,1,0:T(8,128)(2,1)S(1)} %bitcast.250), custom_call_target="tpu_custom_call" | custom-call | bytes 2621440 | tf_op jit(solution)/shard_map/exchange_14/pallas_call | solution.py:158
  562.5 4.9 exchange_15.1
  568.7 5.5 exchange_16.1
  (352 shorter events, 82.5 us)
Async XLA Ops:
  3.5 32.9 %copy-start.83 = (f32[128]{0:T(128)}, f32[128]{0:T(128)S(1)}, u32[]{:S(2)}) copy-start(f32[128]{0:T(128)S(1)} %broadcast_multiply_fusion.11) | copy-start | bytes 1540
  4.8 31.6 %copy-start.87 = (f32[128]{0:T(128)}, f32[128]{0:T(128)S(1)}, u32[]{:S(2)}) copy-start(f32[128]{0:T(128)S(1)} %add_rsqrt_fusion.3) | copy-start | bytes 1540
  36.2 32.2 %copy-start.76 = (f32[4,64]{1,0:T(4,128)}, f32[4,64]{1,0:T(4,128)S(1)}, u32[]{:S(2)}) copy-start(f32[4,64]{1,0:T(4,128)S(1)} %add.253) | copy-start | bytes 3076
  36.3 34.8 %copy-start.78 = (f32[4,64]{1,0:T(4,128)}, f32[4,64]{1,0:T(4,128)S(1)}, u32[]{:S(2)}) copy-start(f32[4,64]{1,0:T(4,128)S(1)} %add.250) | copy-start | bytes 3076
  73.3 25.9 %copy-start.48 = (bf16[4,64,512]{2,1,0:T(8,128)(2,1)}, bf16[4,64,512]{2,1,0:T(8,128)(2,1)S(1)}, u32[]{:S(2)}) copy-start(bf16[4,64,512]{2,1,0:T(8,128)(2,1)S(1)} %convolution_convert_fusion.19) | copy-start | bytes 786436
  73.3 26.1 %copy-start.17 = (f32[128,1024]{1,0:T(8,128)S(1)}, f32[128,1024]{1,0:T(8,128)}, u32[]{:S(2)}) copy-start(f32[128,1024]{1,0:T(8,128)} %param.11) | copy-start | bytes 1572868
  99.6 29.2 %copy-start.85 = (f32[128]{0:T(128)}, f32[128]{0:T(128)S(1)}, u32[]{:S(2)}) copy-start(f32[128]{0:T(128)S(1)} %broadcast_multiply_fusion.10) | copy-start | bytes 1540
  100.6 28.1 %copy-start.89 = (f32[128]{0:T(128)}, f32[128]{0:T(128)S(1)}, u32[]{:S(2)}) copy-start(f32[128]{0:T(128)S(1)} %add_rsqrt_fusion.2) | copy-start | bytes 1540
  133.6 24.9 %copy-start.20 = (f32[128,1024]{1,0:T(8,128)S(1)}, f32[128,1024]{1,0:T(8,128)}, u32[]{:S(2)}) copy-start(f32[128,1024]{1,0:T(8,128)} %copy-done.19) | copy-start | bytes 1572868
  158.5 24.4 %copy-start.46 = (bf16[768,1024]{1,0:T(8,128)(2,1)S(1)}, bf16[768,1024]{1,0:T(8,128)(2,1)}, u32[]{:S(2)}) copy-start(bf16[768,1024]{1,0:T(8,128)(2,1)} %copy.111) | copy-start | bytes 4718596
  158.7 51.8 %copy-start.22 = (f32[128,1024]{1,0:T(8,128)}, f32[128,1024]{1,0:T(8,128)S(1)}, u32[]{:S(2)}) copy-start(f32[128,1024]{1,0:T(8,128)S(1)} %get-tuple-element.143) | copy-start | bytes 1572868
  185.9 146.9 %copy-start.26 = (f32[4,512,512]{1,2,0:T(8,128)}, f32[4,512,512]{1,2,0:T(8,128)S(1)}, u32[]{:S(2)}) copy-start(f32[4,512,512]{1,2,0:T(8,128)S(1)} %get-tuple-element.186) | copy-start | bytes 12582916
  302.9 29.3 %copy-start.51 = (bf16[4,64,512]{2,1,0:T(8,128)(2,1)S(1)}, bf16[4,64,512]{2,1,0:T(8,128)(2,1)}, u32[]{:S(2)}) copy-start(bf16[4,64,512]{2,1,0:T(8,128)(2,1)} %copy-done.50) | copy-start | bytes 786436
  431.4 31.8 %copy-start.21 = (f32[128,1024]{1,0:T(8,128)S(1)}, f32[128,1024]{1,0:T(8,128)}, u32[]{:S(2)}) copy-start(f32[128,1024]{1,0:T(8,128)} %copy-done.19) | copy-start | bytes 1572868
  431.4 31.8 %copy-start.86 = (f32[128]{0:T(128)S(1)}, f32[128]{0:T(128)}, u32[]{:S(2)}) copy-start(f32[128]{0:T(128)} %copy-done.85) | copy-start | bytes 1540
  431.4 31.8 %copy-start.90 = (f32[128]{0:T(128)S(1)}, f32[128]{0:T(128)}, u32[]{:S(2)}) copy-start(f32[128]{0:T(128)} %copy-done.89) | copy-start | bytes 1540
  467.4 30.5 %copy-start.49 = (bf16[4,64,512]{2,1,0:T(8,128)(2,1)S(1)}, bf16[4,64,512]{2,1,0:T(8,128)(2,1)}, u32[]{:S(2)}) copy-start(bf16[4,64,512]{2,1,0:T(8,128)(2,1)} %copy-done.48) | copy-start | bytes 786436
  470.0 28.4 %copy-start.25 = (f32[4,512,512]{1,2,0:T(8,128)S(1)}, f32[4,512,512]{1,2,0:T(8,128)}, u32[]{:S(2)}) copy-start(f32[4,512,512]{1,2,0:T(8,128)} %copy-done.24) | copy-start | bytes 12582916
  528.4 30.4 %copy-start.63 = (f32[1024]{0:T(1024)S(1)}, f32[1024]{0:T(1024)}, u32[]{:S(2)}) copy-start(f32[1024]{0:T(1024)} %get-tuple-element.150) | copy-start | bytes 12292
  528.4 30.4 %copy-start.64 = (f32[1024]{0:T(1024)S(1)}, f32[1024]{0:T(1024)}, u32[]{:S(2)}) copy-start(f32[1024]{0:T(1024)} %get-tuple-element.124) | copy-start | bytes 12292
  528.4 30.4 %copy-start.65 = (f32[1024]{0:T(1024)S(1)}, f32[1024]{0:T(1024)}, u32[]{:S(2)}) copy-start(f32[1024]{0:T(1024)} %get-tuple-element.138) | copy-start | bytes 12292
  528.4 30.4 %copy-start.66 = (f32[1024]{0:T(1024)S(1)}, f32[1024]{0:T(1024)}, u32[]{:S(2)}) copy-start(f32[1024]{0:T(1024)} %get-tuple-element.122) | copy-start | bytes 12292
  528.4 30.4 %copy-start.67 = (f32[1024]{0:T(1024)S(1)}, f32[1024]{0:T(1024)}, u32[]{:S(2)}) copy-start(f32[1024]{0:T(1024)} %get-tuple-element.136) | copy-start | bytes 12292
  528.4 30.4 %copy-start.68 = (f32[1024]{0:T(1024)S(1)}, f32[1024]{0:T(1024)}, u32[]{:S(2)}) copy-start(f32[1024]{0:T(1024)} %get-tuple-element.120) | copy-start | bytes 12292
  528.4 30.4 %copy-start.69 = (f32[1024]{0:T(1024)S(1)}, f32[1024]{0:T(1024)}, u32[]{:S(2)}) copy-start(f32[1024]{0:T(1024)} %get-tuple-element.134) | copy-start | bytes 12292
  528.4 30.4 %copy-start.92 = (f32[4,64]{1,0:T(4,128)S(1)}, f32[4,64]{1,0:T(4,128)}, u32[]{:S(2)}) copy-start(f32[4,64]{1,0:T(4,128)} %get-tuple-element.152) | copy-start | bytes 3076
  528.4 30.5 %copy-start.73 = (f32[1,1,8,32]{3,1,0,2:T(1,128)S(1)}, f32[1,1,8,32]{3,1,0,2:T(1,128)}, u32[]{:S(2)}) copy-start(f32[1,1,8,32]{3,1,0,2:T(1,128)} %stack.147) | copy-start | bytes 3076
  528.5 30.5 %copy-start.74 = (f32[1,1,8,32]{3,1,0,2:T(1,128)S(1)}, f32[1,1,8,32]{3,1,0,2:T(1,128)}, u32[]{:S(2)}) copy-start(f32[1,1,8,32]{3,1,0,2:T(1,128)} %stack.146) | copy-start | bytes 3076
  528.5 30.5 %copy-start.75 = (f32[1,1,8,32]{3,1,0,2:T(1,128)S(1)}, f32[1,1,8,32]{3,1,0,2:T(1,128)}, u32[]{:S(2)}) copy-start(f32[1,1,8,32]{3,1,0,2:T(1,128)} %stack.144) | copy-start | bytes 3076
  528.5 30.6 %copy-start.18 = (f32[128,1024]{1,0:T(8,128)S(1)}, f32[128,1024]{1,0:T(8,128)}, u32[]{:S(2)}) copy-start(f32[128,1024]{1,0:T(8,128)} %param.11) | copy-start | bytes 1572868
  528.5 30.6 %copy-start.84 = (f32[128]{0:T(128)S(1)}, f32[128]{0:T(128)}, u32[]{:S(2)}) copy-start(f32[128]{0:T(128)} %copy-done.83) | copy-start | bytes 1540
  528.5 30.6 %copy-start.88 = (f32[128]{0:T(128)S(1)}, f32[128]{0:T(128)}, u32[]{:S(2)}) copy-start(f32[128]{0:T(128)} %copy-done.87) | copy-start | bytes 1540
  (69 other events, 246.3 us)

commit v2 on v1

--- a/solution.py
+++ b/solution.py
@@ -65,7 +65,8 @@
     count = len(plan)
     ins = refs[:count]
     outs = refs[count : 2 * count]
-    send_sem, recv_sem, own_sem = refs[2 * count :]
+    send_sem, recv_sem, own_sem = refs[2 * count : 2 * count + 3]
+    spare = list(refs[2 * count + 3 :])
 
     greeted = []
     for axis in sorted({axis for axis, _, _ in plan}):
@@ -100,13 +101,98 @@
         copy.start()
         return copy
 
+    def in_line(axis, src, dst, base, place, target, arrival):
+        return pltpu.make_async_remote_copy(
+            src_ref=src,
+            dst_ref=dst,
+            send_sem=send_sem.at[base + place],
+            recv_sem=recv_sem.at[base + arrival],
+            device_id={axis: jnp.int32(target)},
+            device_id_type=pl.DeviceIdType.MESH,
+        )
+
+    def line_start(axis, kind, src, dst, base, held):
+        me = lax.axis_index(axis)
+        for m in range(4):
+
+            @pl.when(me == m)
+            def _(m=m):
+                if kind == "sum" and m in (0, 3):
+                    far = 3 - m
+                    near = 1 if m == 0 else 2
+                    in_line(axis, src.at[far], held, base, far, near, 4).start()
+                for target in ((2, 1), (3, 2, 0), (0, 1, 3), (1, 2))[m]:
+                    if kind == "sum" and (m, target) in ((1, 3), (2, 0)):
+                        continue
+                    block = src.at[target] if kind == "sum" else src
+                    in_line(axis, block, dst.at[m], base, target, target, m).start()
+
+    def line_relay(axis, kind, src, dst, base, held, mixed):
+        me = lax.axis_index(axis)
+        for m in (1, 2):
+
+            @pl.when(me == m)
+            def _(m=m):
+                far = 3 if m == 1 else 0
+                near = 3 - far
+                if kind == "line":
+                    in_line(axis, src, dst.at[far], base, far, far, far).wait_recv()
+                    in_line(axis, dst.at[far], dst.at[far], base, 4, near, far).start()
+                else:
+                    in_line(axis, held, held, base, far, far, 4).wait_recv()
+
+                    def add(row, carry):
+                        rows = pl.ds(row * 16, 16)
+                        mixed[rows] = (
+                            held[rows].astype(jnp.float32)
+                            + src[far, rows].astype(jnp.float32)
+                        ).astype(mixed.dtype)
+                        return carry
+
+                    lax.fori_loop(0, mixed.shape[0] // 16, add, 0)
+                    in_line(axis, mixed, dst.at[m], base, far, far, m).start()
+
+        if kind == "sum":
+            for m in (0, 3):
+
+                @pl.when(me == m)
+                def _(m=m):
+                    dst[3 - m] = jnp.zeros(dst.shape[1:], dst.dtype)
+
+    def line_finish(axis, kind, src, dst, base, held, mixed):
+        me = lax.axis_index(axis)
+        for m in range(4):
+
+            @pl.when(me == m)
+            def _(m=m):
+                block = src.at[0] if kind == "sum" else src
+                for other in range(4):
+                    if other == m:
+                        continue
+                    ends = (m, other) in ((0, 3), (3, 0))
+                    relayed = (m, other) in ((1, 3), (2, 0))
+                    copy = in_line(axis, block, dst.at[other], base, other, other, other)
+                    if not (kind == "sum" and ends) and not (kind == "line" and relayed):
+                        copy.wait_recv()
+                    if not (kind == "line" and ends):
+                        copy.wait_send()
+                if kind == "line" and m in (1, 2):
+                    in_line(axis, block, dst.at[0], base, 4, 0, 0).wait_send()
+
     started = []
     relays = []
     own = []
+    lines = []
     for index, (axis, kind, size) in enumerate(plan):
         me = lax.axis_index(axis)
         src, dst = ins[index], outs[index]
-        if kind == "paired":
+        if kind in ("line", "sum"):
+            held = spare.pop(0) if kind == "sum" else None
+            mixed = spare.pop(0) if kind == "sum" else None
+            line_start(axis, kind, src, dst, used[0], held)
+            lines.append((axis, kind, src, dst, used[0], held, mixed))
+            used[0] += 5
+        elif kind == "paired":
             for k in range(2, size, 2):
                 copy = remote(src, dst.at[me], {axis: (me + k) % size})
                 relays.append((copy, dst, axis, (me + size - k) % size))
@@ -118,10 +204,12 @@
                 started.append(remote(block, dst.at[me], {axis: peer}))
     for index, (axis, kind, size) in enumerate(plan):
         me = lax.axis_index(axis)
-        block = ins[index].at[me] if kind == "swap" else ins[index]
+        block = ins[index].at[me] if kind in ("swap", "sum") else ins[index]
         copy = pltpu.make_async_copy(block, outs[index].at[me], own_sem.at[index])
         copy.start()
         own.append(copy)
+    for line in lines:
+        line_relay(*line)
     for copy, dst, axis, slot in relays:
         copy.wait_recv()
         me = lax.axis_index(axis)
@@ -134,6 +222,8 @@
         copy.wait()
     for copy in started:
         copy.wait()
+    for line in lines:
+        line_finish(*line)
 
 
 def make_exchange():
@@ -144,13 +234,18 @@
         shapes = []
         copies = 0
         sent = 0
+        spare = []
         for axis, kind, value in items:
             size = lax.axis_size(axis)
             if kind == "paired" and size % 2:
                 kind = "gather"
+            block = value.shape[1:] if kind == "swap" else value.shape
+            if axis == "tensor" and size == 4 and value.dtype == jnp.bfloat16:
+                kind = {"swap": "sum", "gather": "line"}[kind]
+                if kind == "sum":
+                    spare += [pltpu.VMEM(block, value.dtype)] * 2
             plan.append((axis, kind, size))
-            copies += size - 1
-            block = value.shape[1:] if kind == "swap" else value.shape
+            copies += 5 if kind in ("line", "sum") else size - 1
             shapes.append(jax.ShapeDtypeStruct((size,) + block, value.dtype))
             sent += (size - 1) * math.prod(block) * value.dtype.itemsize
         collective_id = calls[0]
@@ -164,6 +259,7 @@
                 pltpu.SemaphoreType.DMA((copies,)),
                 pltpu.SemaphoreType.DMA((copies,)),
                 pltpu.SemaphoreType.DMA((len(plan),)),
+                *spare,
             ],
             compiler_params=pltpu.CompilerParams(
                 collective_id=collective_id,
@@ -375,7 +471,9 @@
         if last:
             grad_half = last_grad_half
         else:
-            (grad_half,), _ = step([("gather", back.astype(half))])
+            (grad_half,), (grads["qkv", layer_index + 1],) = step(
+                [("gather", back.astype(half))], sums=[waiting]
+            )
         grad_down = by_owner(contract_first(grad_half, activated))
         grad_pre = (
             jnp.dot(grad_half, weights["down", layer_index], preferred_element_type=jnp.float32)
@@ -385,15 +483,19 @@
         grad_up = by_owner(contract_first(normed_two, grad_pre_half))
         partial = to_owners(contract_last(grad_pre_half, weights["up", layer_index]))
         if last:
-            (grad_normed_two, summed), (grads["down", layer_index],) = step(
-                [partial, ffn_partial], sums=[grad_down]
+            cut = grad_up.shape[2] // 2
+            (grad_normed_two, summed), (grads["down", layer_index], up_left) = step(
+                [partial, ffn_partial], sums=[grad_down, grad_up[:, :, :cut]]
             )
             output = residual_mid + summed + bias_all[layer_index][3]
         else:
             (grad_normed_two,), (grads["down", layer_index],) = step([partial], sums=[grad_down])
         grad_mid = back + norm_back(grad_normed_two, unit_two, inv_two, gain_rows[1])
-        (grad_mid_half,), (grads["up", layer_index],) = step(
-            [("gather", grad_mid.astype(half))], sums=[grad_up]
+        (grad_mid_half,), (up_part,) = step(
+            [("gather", grad_mid.astype(half))], sums=[grad_up[:, :, cut:] if last else grad_up]
+        )
+        grads["up", layer_index] = (
+            jnp.concatenate([up_left, up_part], axis=1) if last else up_part
         )
         grad_out = by_owner(contract_first(grad_mid_half, attended))
         grad_attended = jnp.dot(
@@ -408,10 +510,15 @@
             [part.astype(half).reshape(flat) for part in (query_grad, key_grad, val_grad)], axis=1
         )
         grad_qkv_weight = by_owner(contract_first(normed_one, grad_qkv))
-        (grad_normed_one,), (grads["qkv", layer_index], grads["out", layer_index]) = step(
+        (grad_normed_one,), sent_now = step(
             [to_owners(contract_last(grad_qkv, weights["qkv", layer_index]))],
-            sums=[grad_qkv_weight, grad_out],
-        )
+            sums=[grad_out] if layer_index else [grad_out, grad_qkv_weight],
+        )
+        grads["out", layer_index] = sent_now[0]
+        if layer_index:
+            waiting = grad_qkv_weight
+        else:
+            grads["qkv", layer_index] = sent_now[1]
         small_terms[layer_index] = (
             jnp.stack(
                 [

time: 588 us -> 524 us (0.89)
  Pallas kernels: 426 us -> 364 us
    pallas_call x17, Pallas kernels: 426 us -> 364 us  [exchange(): pl.pallas_call(lambda *refs: exchange_kernel(tuple(plan), *refs), out_sha...]
where the time goes in v2:
time: 524 us; the launch traced here: 515 us
  Pallas kernels  364 us (69%)
  matrix products  89.7 us (17%)
  other arithmetic  33.6 us (6%)
  local copies, waits for them, and re-layouts  25.4 us (5%)
    pallas_call x17, Pallas kernels, exchange(): pl.pallas_call(lambda *refs: exchange_kernel(tuple(plan), *refs), out_sha...  364 us
    dot_general x2, matrix products, attend_back(): jnp.einsum('hqk,khd->qhd', score_grad, key_vecs, preferred_element_type=j...  19.6 us
    dot_general x2, matrix products, attend_back(): jnp.einsum('hqk,qhd->khd', score_grad, queries, preferred_element_type=jn...  15.5 us
    dot_general x8, matrix products, contract_first(): lax.dot_general(left, right, (((0,), (0,)), ((), ())), preferred_element_...  13.6 us
    unnamed x199, local copies, waits for them, and re-layouts  11.4 us
    dot_general x8, matrix products, contract_last(): lax.dot_general(left, right, (((1,), (1,)), ((), ())), preferred_element_...  10.7 us

profile of v2, /device:TPU:0, one launch (start us, length us, event | category | flops | bytes accessed | tf_op | source)
XLA Modules:
  0.0 515.1 jit_solution(16175375750920149177)
XLA Ops:
  9.4 23.9 %exchange_0.1 = (bf16[4,128,1024]{2,1,0:T(8,128)(2,1)S(1)}, bf16[8,16,128]{2,1,0:T(8,128)(2,1)S(1)}, bf16[8,128,768]{2,1,0:T(8,128)(2,1)S(1)}) custom-call(bf16[128,1024]{1,0:T(8,128)(2,1)S(1)} %get-tuple-element.157.refs_0_, bf16[16,128]{1,0:T(8,128)(2,1)S(1)} %fusion.64.refs_1_, bf16[128,768]{1,0:T(8,128)(2,1)S(1)} %copy.101.refs_2_), custom_call_target="tpu_custom_call" | custom-call | bytes 2191360 | tf_op jit(solution)/shard_map/exchange_0/pallas_call | solution.py:253
  37.8 20.1 %exchange_1.1 = (bf16[4,128,1024]{2,1,0:T(8,128)(2,1)S(1)}, bf16[8,128,256]{2,1,0:T(8,128)(2,1)S(1)}, bf16[8,128,1024]{2,1,0:T(8,128)(2,1)S(1)}) custom-call(bf16[128,1024]{1,0:T(8,128)(2,1)S(1)} %add_convert_fusion.7.refs_0_, bf16[128,256]{1,0:T(8,128)(2,1)S(1)} %bitcast.267, bf16[128,1024]{1,0:T(8,128)(2,1)S(1)} %get-tuple-element.170.refs_2_), custom_call_target="tpu_custom_call" | custom-call | bytes 3080192 | tf_op jit(solution)/shard_map/exchange_1/pallas_call | solution.py:253
  57.9 3.6 fusion.102
  67.1 21.1 %exchange_2.1 = (bf16[4,128,1024]{2,1,0:T(8,128)(2,1)S(1)}, bf16[8,128,1024]{2,1,0:T(8,128)(2,1)S(1)}) custom-call(bf16[4,128,1024]{2,1,0:T(8,128)(2,1)S(1)} %bitcast.243, bf16[128,1024]{1,0:T(8,128)(2,1)S(1)} %bitcast.264), custom_call_target="tpu_custom_call" | custom-call | bytes 2621440 | tf_op jit(solution)/shard_map/exchange_2/pallas_call | solution.py:253
  89.9 20.4 %exchange_3.1 = (bf16[4,128,1024]{2,1,0:T(8,128)(2,1)S(1)}, bf16[8,128,768]{2,1,0:T(8,128)(2,1)S(1)}, bf16[8,128,256]{2,1,0:T(8,128)(2,1)S(1)}) custom-call(bf16[128,1024]{1,0:T(8,128)(2,1)S(1)} %add_convert_fusion.4.refs_0_, bf16[128,768]{1,0:T(8,128)(2,1)S(1)} %copy.109.refs_1_, bf16[128,256]{1,0:T(8,128)(2,1)S(1)} %bitcast.269), custom_call_target="tpu_custom_call" | custom-call | bytes 2621440 | tf_op jit(solution)/shard_map/exchange_3/pallas_call | solution.py:253
  112.9 3.3 fusion.103
  117.8 21.1 %exchange_4.1 = (bf16[4,128,1024]{2,1,0:T(8,128)(2,1)S(1)}, bf16[8,128,1024]{2,1,0:T(8,128)(2,1)S(1)}) custom-call(bf16[4,128,1024]{2,1,0:T(8,128)(2,1)S(1)} %bitcast.263, bf16[128,1024]{1,0:T(8,128)(2,1)S(1)} %get-tuple-element.169.refs_1_), custom_call_target="tpu_custom_call" | custom-call | bytes 2621440 | tf_op jit(solution)/shard_map/exchange_4/pallas_call | solution.py:253
  139.6 19.9 %exchange_5.1 = (bf16[4,128,1024]{2,1,0:T(8,128)(2,1)S(1)}, bf16[8,128,1024]{2,1,0:T(8,128)(2,1)S(1)}) custom-call(bf16[128,1024]{1,0:T(8,128)(2,1)S(1)} %add_convert_fusion.3.refs_0_, bf16[128,1024]{1,0:T(8,128)(2,1)S(1)} %bitcast.266), custom_call_target="tpu_custom_call" | custom-call | bytes 2621440 | tf_op jit(solution)/shard_map/exchange_5/pallas_call | solution.py:253
  165.1 20.3 %exchange_6.1 = bf16[4,128,1024]{2,1,0:T(8,128)(2,1)S(1)} custom-call(bf16[4,128,1024]{2,1,0:T(8,128)(2,1)S(1)} %bitcast.244), custom_call_target="tpu_custom_call" | custom-call | bytes 786432 | tf_op jit(solution)/shard_map/exchange_6/pallas_call | solution.py:253
  186.2 19.1 %exchange_7.1 = bf16[4,128,1024]{2,1,0:T(8,128)(2,1)S(1)} custom-call(bf16[128,1024]{1,0:T(8,128)(2,1)S(1)} %add_convert_fusion.refs_0_), custom_call_target="tpu_custom_call" | custom-call | bytes 786432 | tf_op jit(solution)/shard_map/exchange_7/pallas_call | solution.py:253
  208.1 2.9 fusion.100
  211.0 2.8 convolution_convert_fusion.3
  217.5 42.8 %exchange_8.1 = (bf16[4,128,1024]{2,1,0:T(8,128)(2,1)S(1)}, bf16[4,128,1024]{2,1,0:T(8,128)(2,1)S(1)}, bf16[8,128,1024]{2,1,0:T(8,128)(2,1)}, bf16[8,128,512]{2,1,0:T(8,128)(2,1)S(1)}) custom-call(bf16[4,128,1024]{2,1,0:T(8,128)(2,1)S(1)} %bitcast.258, bf16[4,128,1024]{2,1,0:T(8,128)(2,1)S(1)} %bitcast.257, bf16[8,128,1024]{2,1,0:T(8,128)(2,1)} %bitcast.290, ...), custom_call_target="tpu_custom_call" | custom-call | bytes 4325376 | tf_op jit(solution)/shard_map/exchange_8/pallas_call | solution.py:253
  265.1 20.4 %exchange_9.1 = (bf16[4,128,1024]{2,1,0:T(8,128)(2,1)S(1)}, bf16[8,128,512]{2,1,0:T(8,128)(2,1)S(1)}) custom-call(bf16[128,1024]{1,0:T(8,128)(2,1)S(1)} %convert_element_type.318.refs_0_, bf16[8,128,512]{2,1,0:T(8,128)(2,1)S(1)} %get-tuple-element.150.refs_1_), custom_call_target="tpu_custom_call" | custom-call | bytes 1703936 | tf_op jit(solution)/shard_map/exchange_9/pallas_call | solution.py:253
  290.2 4.1 fusion.53
  294.2 8.1 %fusion.39 = bf16[4,64,512]{2,1,0:T(8,128)(2,1)} fusion(f32[4,512,512]{1,2,0:T(8,128)} %fusion.53, f32[512,4,64]{0,2,1:T(8,128)S(1)} %bitcast.298, f32[4,64]{1,0:T(4,128)S(1)} %add.281, f32[4,512,512]{1,2,0:T(8,128)} %copy-done.24, f32[4,512]{1,0:T(4,128)S(1)} %log_add_fusion, pred[512,512]{0,1:T(8,128)(4,1)S(1)} %copy-done.26), kind=kOutput, calls=%fused_computation.74 | convolution fusion | flops 146147840 | bytes 9446400 | tf_op jit(solution)/shard_map/hqk,qhd->khd/dot_general | solution.py:312
  302.4 9.6 %fusion.89 = (f32[4,64]{1,0:T(4,128)S(1)}, bf16[512,4,64]{0,2,1:T(8,128)(2,1)}) fusion(bf16[512,4,64]{0,2,1:T(8,128)(2,1)} %bitcast.319, f32[4,512,512]{1,2,0:T(8,128)} %fusion.53, f32[4,512]{1,0:T(4,128)S(1)} %log_add_fusion, f32[4,512,512]{1,2,0:T(8,128)} %copy-done.24, pred[512,512]{0,1:T(8,128)(4,1)S(1)} %copy-done.26), kind=kOutput, calls=%fused_computation.218 | convolution fusion | flops 146016512 | bytes 9184256 | tf_op jit(solution)/shard_map/hqk,khd->qhd/dot_general | solution.py:309
  315.1 21.4 %exchange_10.1 = (bf16[4,128,1024]{2,1,0:T(8,128)(2,1)S(1)}, bf16[8,128,256]{2,1,0:T(8,128)(2,1)S(1)}) custom-call(bf16[4,128,1024]{2,1,0:T(8,128)(2,1)S(1)} %bitcast.265, bf16[8,128,256]{2,1,0:T(8,128)(2,1)S(1)} %bitcast.249), custom_call_target="tpu_custom_call" | custom-call | bytes 1245184 | tf_op jit(solution)/shard_map/exchange_10/pallas_call | solution.py:253
  340.4 2.2 fusion.78
  342.7 20.4 %exchange_11.1 = (bf16[4,128,1024]{2,1,0:T(8,128)(2,1)S(1)}, bf16[8,128,768]{2,1,0:T(8,128)(2,1)S(1)}) custom-call(bf16[128,1024]{1,0:T(8,128)(2,1)S(1)} %convert_element_type.328.refs_0_, bf16[8,128,768]{2,1,0:T(8,128)(2,1)S(1)} %bitcast.256), custom_call_target="tpu_custom_call" | custom-call | bytes 2162688 | tf_op jit(solution)/shard_map/exchange_11/pallas_call | solution.py:253
  363.1 2.2 fusion.101
  365.4 2.8 convolution_convert_fusion.1
  369.5 27.3 %exchange_12.1 = (bf16[4,128,1024]{2,1,0:T(8,128)(2,1)S(1)}, bf16[8,128,1024]{2,1,0:T(8,128)(2,1)S(1)}) custom-call(bf16[4,128,1024]{2,1,0:T(8,128)(2,1)S(1)} %bitcast.260, bf16[8,128,1024]{2,1,0:T(8,128)(2,1)} %bitcast.289), custom_call_target="tpu_custom_call" | custom-call | bytes 2621440 | tf_op jit(solution)/shard_map/exchange_12/pallas_call | solution.py:253
  405.6 2.6 convolution_convert_fusion
  408.2 26.5 %exchange_13.1 = (bf16[4,128,1024]{2,1,0:T(8,128)(2,1)S(1)}, bf16[8,128,1024]{2,1,0:T(8,128)(2,1)S(1)}) custom-call(bf16[128,1024]{1,0:T(8,128)(2,1)S(1)} %convert_element_type.334.refs_0_, bf16[8,128,1024]{2,1,0:T(8,128)(2,1)S(1)} %bitcast.250), custom_call_target="tpu_custom_call" | custom-call | bytes 2621440 | tf_op jit(solution)/shard_map/exchange_13/pallas_call | solution.py:253
  440.8 2.9 fusion.51
  443.7 7.4 %fusion.36 = bf16[4,64,512]{2,1,0:T(8,128)(2,1)S(1)} fusion(f32[4,512,512]{1,2,0:T(8,128)} %fusion.51, f32[512,4,64]{0,2,1:T(8,128)S(1)} %bitcast.293, f32[4,64]{1,0:T(4,128)S(1)} %copy-done.70, f32[4,512,512]{1,2,0:T(8,128)} %copy-done.22, f32[4,512]{1,0:T(4,128)S(1)} %copy-done.75, pred[512,512]{0,1:T(8,128)(4,1)S(1)} %copy-done.26), kind=kOutput, calls=%fused_computation.73 | convolution fusion | flops 146147840 | bytes 9446400 | tf_op jit(solution)/shard_map/hqk,qhd->khd/dot_general | solution.py:312
  451.1 10.0 %fusion.87 = (f32[4,64]{1,0:T(4,128)}, bf16[512,4,64]{0,2,1:T(8,128)(2,1)}) fusion(bf16[512,4,64]{0,2,1:T(8,128)(2,1)S(1)} %bitcast.317, f32[4,512,512]{1,2,0:T(8,128)} %fusion.51, f32[4,512]{1,0:T(4,128)S(1)} %copy-done.75, f32[4,512,512]{1,2,0:T(8,128)} %copy-done.22, pred[512,512]{0,1:T(8,128)(4,1)S(1)} %copy-done.26), kind=kOutput, calls=%fused_computation.216 | convolution fusion | flops 146016512 | bytes 9184256 | tf_op jit(solution)/shard_map/hqk,khd->qhd/dot_general | solution.py:309
  463.3 2.2 convolution_convert_fusion.4
  465.6 27.7 %exchange_14.1 = (bf16[4,128,1024]{2,1,0:T(8,128)(2,1)S(1)}, bf16[8,128,256]{2,1,0:T(8,128)(2,1)S(1)}, bf16[8,128,768]{2,1,0:T(8,128)(2,1)S(1)}) custom-call(bf16[4,128,1024]{2,1,0:T(8,128)(2,1)S(1)} %bitcast.259, bf16[8,128,256]{2,1,0:T(8,128)(2,1)S(1)} %bitcast.251, bf16[8,128,768]{2,1,0:T(8,128)(2,1)} %bitcast.304), custom_call_target="tpu_custom_call" | custom-call | bytes 2621440 | tf_op jit(solution)/shard_map/exchange_14/pallas_call | solution.py:253
  498.2 6.0 %exchange_15.1 = f32[8,16,128]{2,1,0:T(8,128)S(1)} custom-call(f32[8,16,128]{2,1,0:T(8,128)S(1)} %bitcast.268), custom_call_target="tpu_custom_call" | custom-call | bytes 57344 | tf_op jit(solution)/shard_map/exchange_15/pallas_call | solution.py:253
  505.4 5.5 %exchange_16.1 = f32[4,16,128]{2,1,0:T(8,128)S(1)} custom-call(f32[16,128]{1,0:T(8,128)S(1)} %reduce_sum.571.refs_0_), custom_call_target="tpu_custom_call" | custom-call | bytes 24576 | tf_op jit(solution)/shard_map/exchange_16/pallas_call | solution.py:253
  (341 shorter events, 82.2 us)
Async XLA Ops:
  3.5 31.5 %copy-start.76 = (f32[128]{0:T(128)}, f32[128]{0:T(128)S(1)}, u32[]{:S(2)}) copy-start(f32[128]{0:T(128)S(1)} %broadcast_multiply_fusion.11) | copy-start | bytes 1540
  4.8 30.2 %copy-start.80 = (f32[128]{0:T(128)}, f32[128]{0:T(128)S(1)}, u32[]{:S(2)}) copy-start(f32[128]{0:T(128)S(1)} %add_rsqrt_fusion.3) | copy-start | bytes 1540
  34.8 26.8 %copy-start.69 = (f32[4,64]{1,0:T(4,128)}, f32[4,64]{1,0:T(4,128)S(1)}, u32[]{:S(2)}) copy-start(f32[4,64]{1,0:T(4,128)S(1)} %add.253) | copy-start | bytes 3076
  34.9 29.5 %copy-start.71 = (f32[4,64]{1,0:T(4,128)}, f32[4,64]{1,0:T(4,128)S(1)}, u32[]{:S(2)}) copy-start(f32[4,64]{1,0:T(4,128)S(1)} %add.250) | copy-start | bytes 3076
  66.6 21.7 %copy-start.43 = (bf16[4,64,512]{2,1,0:T(8,128)(2,1)}, bf16[4,64,512]{2,1,0:T(8,128)(2,1)S(1)}, u32[]{:S(2)}) copy-start(bf16[4,64,512]{2,1,0:T(8,128)(2,1)S(1)} %convolution_convert_fusion.19) | copy-start | bytes 786436
  66.6 21.9 %copy-start.15 = (f32[128,1024]{1,0:T(8,128)S(1)}, f32[128,1024]{1,0:T(8,128)}, u32[]{:S(2)}) copy-start(f32[128,1024]{1,0:T(8,128)} %param.11) | copy-start | bytes 1572868
  88.7 24.3 %copy-start.78 = (f32[128]{0:T(128)}, f32[128]{0:T(128)S(1)}, u32[]{:S(2)}) copy-start(f32[128]{0:T(128)S(1)} %broadcast_multiply_fusion.10) | copy-start | bytes 1540
  89.7 23.2 %copy-start.82 = (f32[128]{0:T(128)}, f32[128]{0:T(128)S(1)}, u32[]{:S(2)}) copy-start(f32[128]{0:T(128)S(1)} %add_rsqrt_fusion.2) | copy-start | bytes 1540
  117.8 21.3 %copy-start.18 = (f32[128,1024]{1,0:T(8,128)S(1)}, f32[128,1024]{1,0:T(8,128)}, u32[]{:S(2)}) copy-start(f32[128,1024]{1,0:T(8,128)} %copy-done.17) | copy-start | bytes 1572868
  139.2 46.4 %copy-start.20 = (f32[128,1024]{1,0:T(8,128)}, f32[128,1024]{1,0:T(8,128)S(1)}, u32[]{:S(2)}) copy-start(f32[128,1024]{1,0:T(8,128)S(1)} %get-tuple-element.147) | copy-start | bytes 1572868
  162.4 125.1 %copy-start.24 = (f32[4,512,512]{1,2,0:T(8,128)}, f32[4,512,512]{1,2,0:T(8,128)S(1)}, u32[]{:S(2)}) copy-start(f32[4,512,512]{1,2,0:T(8,128)S(1)} %get-tuple-element.192) | copy-start | bytes 12582916
  164.6 21.0 %copy-start.45 = (bf16[4,64,512]{2,1,0:T(8,128)(2,1)}, bf16[4,64,512]{2,1,0:T(8,128)(2,1)S(1)}, u32[]{:S(2)}) copy-start(bf16[4,64,512]{2,1,0:T(8,128)(2,1)S(1)} %convolution_convert_fusion.18) | copy-start | bytes 786436
  340.4 22.7 %copy-start.92 = (f32[512,1024]{1,0:T(8,128)S(1)}, f32[512,1024]{1,0:T(8,128)}, u32[]{:S(2)}) copy-start(f32[512,1024]{1,0:T(8,128)} %copy-done.91) | copy-start | bytes 6291460
  369.5 28.3 %copy-start.19 = (f32[128,1024]{1,0:T(8,128)S(1)}, f32[128,1024]{1,0:T(8,128)}, u32[]{:S(2)}) copy-start(f32[128,1024]{1,0:T(8,128)} %copy-done.17) | copy-start | bytes 1572868
  369.5 28.3 %copy-start.79 = (f32[128]{0:T(128)S(1)}, f32[128]{0:T(128)}, u32[]{:S(2)}) copy-start(f32[128]{0:T(128)} %copy-done.78) | copy-start | bytes 1540
  369.5 28.3 %copy-start.83 = (f32[128]{0:T(128)S(1)}, f32[128]{0:T(128)}, u32[]{:S(2)}) copy-start(f32[128]{0:T(128)} %copy-done.82) | copy-start | bytes 1540
  405.6 29.6 %copy-start.44 = (bf16[4,64,512]{2,1,0:T(8,128)(2,1)S(1)}, bf16[4,64,512]{2,1,0:T(8,128)(2,1)}, u32[]{:S(2)}) copy-start(bf16[4,64,512]{2,1,0:T(8,128)(2,1)} %copy-done.43) | copy-start | bytes 786436
  408.2 27.5 %copy-start.23 = (f32[4,512,512]{1,2,0:T(8,128)S(1)}, f32[4,512,512]{1,2,0:T(8,128)}, u32[]{:S(2)}) copy-start(f32[4,512,512]{1,2,0:T(8,128)} %copy-done.22) | copy-start | bytes 12582916
  465.5 29.0 %copy-start.56 = (f32[1024]{0:T(1024)S(1)}, f32[1024]{0:T(1024)}, u32[]{:S(2)}) copy-start(f32[1024]{0:T(1024)} %get-tuple-element.156) | copy-start | bytes 12292
  465.5 29.0 %copy-start.57 = (f32[1024]{0:T(1024)S(1)}, f32[1024]{0:T(1024)}, u32[]{:S(2)}) copy-start(f32[1024]{0:T(1024)} %get-tuple-element.128) | copy-start | bytes 12292
  465.5 29.0 %copy-start.58 = (f32[1024]{0:T(1024)S(1)}, f32[1024]{0:T(1024)}, u32[]{:S(2)}) copy-start(f32[1024]{0:T(1024)} %get-tuple-element.142) | copy-start | bytes 12292
  465.5 29.0 %copy-start.59 = (f32[1024]{0:T(1024)S(1)}, f32[1024]{0:T(1024)}, u32[]{:S(2)}) copy-start(f32[1024]{0:T(1024)} %get-tuple-element.126) | copy-start | bytes 12292
  465.5 29.0 %copy-start.60 = (f32[1024]{0:T(1024)S(1)}, f32[1024]{0:T(1024)}, u32[]{:S(2)}) copy-start(f32[1024]{0:T(1024)} %get-tuple-element.140) | copy-start | bytes 12292
  465.5 29.0 %copy-start.61 = (f32[1024]{0:T(1024)S(1)}, f32[1024]{0:T(1024)}, u32[]{:S(2)}) copy-start(f32[1024]{0:T(1024)} %get-tuple-element.124) | copy-start | bytes 12292
  465.5 29.0 %copy-start.62 = (f32[1024]{0:T(1024)S(1)}, f32[1024]{0:T(1024)}, u32[]{:S(2)}) copy-start(f32[1024]{0:T(1024)} %get-tuple-element.138) | copy-start | bytes 12292
  465.5 29.0 %copy-start.85 = (f32[4,64]{1,0:T(4,128)S(1)}, f32[4,64]{1,0:T(4,128)}, u32[]{:S(2)}) copy-start(f32[4,64]{1,0:T(4,128)} %get-tuple-element.158) | copy-start | bytes 3076
  465.5 29.1 %copy-start.66 = (f32[1,1,8,32]{3,1,0,2:T(1,128)S(1)}, f32[1,1,8,32]{3,1,0,2:T(1,128)}, u32[]{:S(2)}) copy-start(f32[1,1,8,32]{3,1,0,2:T(1,128)} %stack.147) | copy-start | bytes 3076
  465.5 29.1 %copy-start.67 = (f32[1,1,8,32]{3,1,0,2:T(1,128)S(1)}, f32[1,1,8,32]{3,1,0,2:T(1,128)}, u32[]{:S(2)}) copy-start(f32[1,1,8,32]{3,1,0,2:T(1,128)} %stack.146) | copy-start | bytes 3076
  465.5 29.1 %copy-start.68 = (f32[1,1,8,32]{3,1,0,2:T(1,128)S(1)}, f32[1,1,8,32]{3,1,0,2:T(1,128)}, u32[]{:S(2)}) copy-start(f32[1,1,8,32]{3,1,0,2:T(1,128)} %stack.144) | copy-start | bytes 3076
  465.5 29.2 %copy-start.16 = (f32[128,1024]{1,0:T(8,128)S(1)}, f32[128,1024]{1,0:T(8,128)}, u32[]{:S(2)}) copy-start(f32[128,1024]{1,0:T(8,128)} %param.11) | copy-start | bytes 1572868
  465.5 29.2 %copy-start.77 = (f32[128]{0:T(128)S(1)}, f32[128]{0:T(128)}, u32[]{:S(2)}) copy-start(f32[128]{0:T(128)} %copy-done.76) | copy-start | bytes 1540
  465.6 29.2 %copy-start.81 = (f32[128]{0:T(128)S(1)}, f32[128]{0:T(128)}, u32[]{:S(2)}) copy-start(f32[128]{0:T(128)} %copy-done.80) | copy-start | bytes 1540
  (62 other events, 236.7 us)
